TPU v7x, 32 devices: a whole 2x2x4 slice. The times are simulated.
32 devices in a mesh: grp: 2 (over y), atoms: 4 (over z), feat: 2 (over x), rep: 2 (over core).
Axes of the slice: x: 2, y: 2, z: 4, core: 2. Of those that a mesh axis runs over, the one named last changes fastest.
Arguments:
- atom_coords: bfloat16 [4, 2048, 3, 3072], P(('grp', 'rep'), None, None, 'atoms'), parts along dimension 0, may hold values from -9 to 9
- atom_pairs: int32 [2, 1024], P(None, 'feat'), may hold values from 0 to 3071, as said below
- traj_ids: int32 [4, 2048], P(('grp', 'rep')), parts along dimension 0, may hold values from 0 to 7, never falling along the last dimension, each value on 1 to 512 neighbouring positions
Outputs:
- corr_inst: float32 [2048, 1024], P(('grp', 'atoms', 'rep'), 'feat'), parts along dimension 0
- corr_lag: float32 [2048, 1024], P(('grp', 'atoms', 'rep'), 'feat'), parts along dimension 0
- projections: float32 [4, 2048, 1024], P(('grp', 'rep'), 'atoms', 'feat'), parts along dimension 0
There are 2 independent parts, one for each index of `grp`. A program takes and returns all parts, laid end to end along the dimension named above; an argument that names none is the same for every part. Nothing has to cross between parts.
Inputs may be any that keep to these rules, and one draw needn't show every extreme that they name: `atom_pairs`: the two atoms of a feature differ. `traj_ids`: trajectory numbers never fall along a replica stream; some trajectory holds exactly 512 frames.
All inputs are finite; a program needn't handle non-finite values.
Results may differ from a plain program's by a relative error of at most 0.0003.
Values may be sent and summed in bfloat16 or wider, within the bound.
A program may use at most 128 MiB of HBM per device.

v0:
```python
import functools
import math

import jax
import jax.numpy as jnp
from jax import lax
from jax.experimental import pallas as pl
from jax.experimental.pallas import tpu as pltpu
from jax.sharding import PartitionSpec as P

LAG = 10
HALO = 16


def matmul(left, right, dims, precision=None):
    return lax.dot_general(
        left, right, (dims, ((), ())), precision=precision, preferred_element_type=jnp.float32
    )

MESH = pl.DeviceIdType.MESH


def exchange_kernel(
    groups, feat_groups, room, lanes, chunks, tile, coords, picked, slots, out, halo, *scratch
):
    blocks, pick, chosen, sign, recv, edge, load, z_send, z_recv, z_own, x_send, x_recv, h_send, h_recv = scratch
    z, x = lax.axis_index("atoms"), lax.axis_index("feat")
    half = groups // 2
    z_steps = [half] + [o for o in range(groups - 1, 0, -1) if o != half] if groups > 1 else []
    x_steps = list(range(1, feat_groups))
    tiles = out.shape[0] // tile
    frames_here = feat_groups * chunks * lanes
    cols = halo.shape[1]
    z_dests = [lax.rem(z + o, groups) for o in z_steps] + [z]
    loads = []
    for ch in range(chunks):
        row = []
        for i, dest in enumerate(z_dests):
            start = pl.multiple_of(dest * frames_here + (x * chunks + ch) * lanes, 16)
            row.append(
                pltpu.make_async_copy(coords.at[:, pl.ds(start, lanes), :], blocks.at[ch, i], load.at[ch, i])
            )
            row[-1].start()
        loads.append(row)
    barrier = pltpu.get_barrier_semaphore()
    for o in z_steps:
        pl.semaphore_signal(barrier, 1, device_id={"atoms": lax.rem(z + o, groups)}, device_id_type=MESH)
    for o in x_steps:
        pl.semaphore_signal(barrier, 1, device_id={"feat": lax.rem(x + o, feat_groups)}, device_id_type=MESH)
    z_up, z_down = lax.rem(z + 1, groups), lax.rem(z + groups - 1, groups)

    @pl.when(x == 0)
    def _():
        for k in x_steps:
            pl.semaphore_signal(barrier, 1, device_id={"atoms": z_down, "feat": k}, device_id_type=MESH)

    @pl.when(x != 0)
    def _():
        pl.semaphore_signal(barrier, 1, device_id={"atoms": z_up, "feat": 0}, device_id_type=MESH)

    width = picked.shape[1]
    slot_no = lax.broadcasted_iota(jnp.int32, (room, width), 0)
    pick[...] = jnp.where(slot_no == picked[...], 1.0, 0.0).astype(jnp.bfloat16)

    @pl.when(x == 0)
    def _():
        pl.semaphore_wait(barrier, len(z_steps) + 2 * len(x_steps))

    @pl.when(x != 0)
    def _():
        pl.semaphore_wait(barrier, len(z_steps) + len(x_steps) + 1)

    def fill(ch, i):
        loads[ch][i].wait()
        for c in range(3):
            got = lax.dot_general(
                pick[...], blocks[ch, i, c], (((1,), (1,)), ((), ())), preferred_element_type=jnp.float32
            )
            chosen[ch, i, :, c * lanes : (c + 1) * lanes] = got.astype(jnp.bfloat16)

    here = pl.ds(pl.multiple_of(z * room, 16), room)
    z_copies = []
    for ch in range(chunks):
        row = []
        for i, o in enumerate(z_steps):
            fill(ch, i)
            row.append(
                pltpu.make_async_remote_copy(
                    src_ref=chosen.at[ch, i],
                    dst_ref=recv.at[ch, here],
                    send_sem=z_send.at[ch, i],
                    recv_sem=z_recv.at[ch, i],
                    device_id={"atoms": z_dests[i]},
                    device_id_type=MESH,
                )
            )
            row[-1].start()
        z_copies.append(row)
    own_copies = []
    for ch in range(chunks):
        fill(ch, len(z_steps))
        own_copies.append(
            pltpu.make_async_copy(chosen.at[ch, len(z_steps)], recv.at[ch, here], z_own.at[ch])
        )
        own_copies[-1].start()

    place = lax.broadcasted_iota(jnp.int32, (128, groups * room), 1)

    def make_sign(i, carry):
        rows = pl.ds(pl.multiple_of(i * 128, 128), 128)
        pair = slots[rows, :]
        value = jnp.where(place == pair[:, 0:1], 1.0, 0.0) - jnp.where(place == pair[:, 1:2], 1.0, 0.0)
        sign[rows, :] = value.astype(jnp.bfloat16)
        return carry

    lax.fori_loop(0, out.shape[0] // 128, make_sign, 0)

    def x_copy(ch, i, k, o):
        part = out.at[
            pl.ds(pl.multiple_of(i * tile, tile), tile),
            pl.ds(pl.multiple_of((x * chunks + ch) * lanes, lanes), lanes),
        ]
        return pltpu.make_async_remote_copy(
            src_ref=part,
            dst_ref=part,
            send_sem=x_send.at[ch, i, k],
            recv_sem=x_recv.at[ch, i, k],
            device_id={"feat": lax.rem(x + o, feat_groups)},
            device_id_type=MESH,
        )

    def h_copy(k):
        return pltpu.make_async_remote_copy(
            src_ref=edge.at[:, k * cols : (k + 1) * cols],
            dst_ref=halo,
            send_sem=h_send.at[k],
            recv_sem=h_recv.at[0],
            device_id={"atoms": z_down, "feat": k},
            device_id_type=MESH,
        )

    for ch in range(chunks):
        own_copies[ch].wait()
        for copy in z_copies[ch]:
            copy.wait_recv()

        def features(i, carry, ch=ch):
            rows = pl.ds(pl.multiple_of(i * tile, tile), tile)
            delta = jnp.dot(sign[rows, :], recv[ch], preferred_element_type=jnp.float32)
            square = delta * delta
            total = square[:, :lanes] + square[:, lanes : 2 * lanes] + square[:, 2 * lanes :]
            cols = pl.ds(pl.multiple_of((x * chunks + ch) * lanes, lanes), lanes)
            out[rows, cols] = jnp.sqrt(total + 0.01)
            for k, o in enumerate(x_steps):
                x_copy(ch, i, k, o).start()
            return carry

        lax.fori_loop(0, tiles, features, 0)
        if ch == 0:

            @pl.when(x == 0)
            def _():
                for i in range(tiles):
                    first = out[i * tile : (i + 1) * tile, :lanes]
                    edge[:, i * tile : (i + 1) * tile] = first.T[:HALO]
                for k in range(feat_groups):
                    h_copy(k).start()

    @pl.when(x == 0)
    def _():
        for k in range(feat_groups):
            h_copy(k).wait_send()

    h_copy(0).wait_recv()
    for ch in range(chunks):
        for copy in z_copies[ch]:
            copy.wait_send()

        def finish(i, carry, ch=ch):
            for k, o in enumerate(x_steps):
                x_copy(ch, i, k, o).wait()
            return carry

        lax.fori_loop(0, tiles, finish, 0)


def exchange(coords, picked, slots, room, lanes, groups, feat_groups):
    feats, width = slots.shape[0], picked.shape[1]
    chunks = coords.shape[1] // (groups * feat_groups * lanes)
    tile = min(256, feats)
    vmem = pl.BlockSpec(memory_space=pltpu.VMEM)
    z_count, x_count = max(groups - 1, 1), max(feat_groups - 1, 1)
    dma = pltpu.SemaphoreType.DMA
    return pl.pallas_call(
        functools.partial(exchange_kernel, groups, feat_groups, room, lanes, chunks, tile),
        out_shape=(
            jax.ShapeDtypeStruct((feats, feat_groups * chunks * lanes), jnp.float32),
            jax.ShapeDtypeStruct((HALO, feats // feat_groups), jnp.float32),
        ),
        in_specs=[pl.BlockSpec(memory_space=pl.ANY), vmem, vmem],
        out_specs=(vmem, vmem),
        scratch_shapes=[
            pltpu.VMEM((chunks, groups, 3, lanes, width), jnp.bfloat16),
            pltpu.VMEM((room, width), jnp.bfloat16),
            pltpu.VMEM((chunks, groups, room, 3 * lanes), jnp.bfloat16),
            pltpu.VMEM((feats, groups * room), jnp.bfloat16),
            pltpu.VMEM((chunks, groups * room, 3 * lanes), jnp.bfloat16),
            pltpu.VMEM((HALO, feats), jnp.float32),
            dma((chunks, groups)),
            dma((chunks, z_count)),
            dma((chunks, z_count)),
            dma((chunks,)),
            dma((chunks, feats // tile, x_count)),
            dma((chunks, feats // tile, x_count)),
            dma((feat_groups,)),
            dma((1,)),
        ],
        compiler_params=pltpu.CompilerParams(
            collective_id=0, has_side_effects=True, vmem_limit_bytes=48 * 1024 * 1024
        ),
    )(coords, picked, slots)


def reduce_kernel(groups, reps, local, stats, out, gathered, core, sums, left, right, *sems):
    c_send, c_recv, s_own, s_send, s_recv, z_send, l_recv, r_recv = sems
    z, r = lax.axis_index("atoms"), lax.axis_index("rep")
    peers = [(a, b) for a in range(groups) for b in range(reps) if (a, b) != (0, 0)]
    barrier = pltpu.get_barrier_semaphore()

    def peer(a, b):
        return {"atoms": lax.rem(z + a, groups), "rep": lax.rem(r + b, reps)}

    for a, b in peers:
        pl.semaphore_signal(barrier, 1, device_id=peer(a, b), device_id_type=MESH)
    pl.semaphore_wait(barrier, len(peers))

    order = []
    for k in range((groups + 1) // 2):
        order += [groups - 1 - k] + ([k] if k != groups - 1 - k else [])
    core_copies = {}
    for d in order:
        for b in range(1, reps):
            core_copies[d, b] = pltpu.make_async_remote_copy(
                src_ref=local.at[d, lax.rem(r + b, reps)],
                dst_ref=core.at[b - 1, d],
                send_sem=c_send.at[b - 1, d],
                recv_sem=c_recv.at[b - 1, d],
                device_id={"rep": lax.rem(r + b, reps)},
                device_id_type=MESH,
            )
            core_copies[d, b].start()
    me = z * reps + r
    own = pltpu.make_async_copy(stats, gathered.at[me], s_own.at[0])
    own.start()
    stat_copies = []
    for k, (a, b) in enumerate(peers):
        stat_copies.append(
            pltpu.make_async_remote_copy(
                src_ref=stats,
                dst_ref=gathered.at[me],
                send_sem=s_send.at[k],
                recv_sem=s_recv.at[k],
                device_id=peer(a, b),
                device_id_type=MESH,
            )
        )
        stat_copies[-1].start()


    def hop(d, step):
        return pltpu.make_async_remote_copy(
            src_ref=sums.at[d],
            dst_ref=(left if step > 0 else right).at[d],
            send_sem=z_send.at[d],
            recv_sem=(l_recv if step > 0 else r_recv).at[d],
            device_id={"atoms": lax.rem(z + step + groups, groups)},
            device_id_type=MESH,
        )

    for d in order:
        total = local[d, r]
        for b in range(1, reps):
            core_copies[d, b].wait_recv()
            total = total + core[b - 1, d]
        sums[d] = total

        if d > 0:

            @pl.when(z == 0)
            def _(d=d):
                hop(d, 1).start()

        if d < groups - 1:

            @pl.when(z == groups - 1)
            def _(d=d):
                hop(d, -1).start()

    for k in range(groups):
        up, down = groups - 1 - k, k

        @pl.when((z > 0) & (z < up))
        def _(d=up):
            hop(d, 1).wait_recv()
            sums[d] = sums[d] + left[d]
            hop(d, 1).start()

        @pl.when((z < groups - 1) & (z > down))
        def _(d=down):
            hop(d, -1).wait_recv()
            sums[d] = sums[d] + right[d]
            hop(d, -1).start()

    for d in range(groups):

        @pl.when(z == d)
        def _(d=d):
            total = sums[d]
            if d > 0:
                hop(d, 1).wait_recv()
                total = total + left[d]
            if d < groups - 1:
                hop(d, -1).wait_recv()
                total = total + right[d]
            out[...] = total

        @pl.when(z < d)
        def _(d=d):
            hop(d, 1).wait_send()

        @pl.when(z > d)
        def _(d=d):
            hop(d, -1).wait_send()

    for copy in core_copies.values():
        copy.wait_send()
    own.wait()
    for copy in stat_copies:
        copy.wait()


def reduce_blocks(local, stats, groups, reps):
    rows, width = local.shape[0] // (groups * reps), local.shape[1]
    vmem = pl.BlockSpec(memory_space=pltpu.VMEM)
    dma = pltpu.SemaphoreType.DMA
    block = pltpu.VMEM((groups, rows, width), jnp.float32)
    others = max(groups * reps - 1, 1)
    others_core = max(reps - 1, 1)
    return pl.pallas_call(
        functools.partial(reduce_kernel, groups, reps),
        out_shape=(
            jax.ShapeDtypeStruct((rows, width), jnp.float32),
            jax.ShapeDtypeStruct((groups * reps,) + stats.shape, jnp.float32),
        ),
        in_specs=[vmem, vmem],
        out_specs=(vmem, vmem),
        scratch_shapes=[
            pltpu.VMEM((others_core, groups, rows, width), jnp.float32),
            block,
            block,
            block,
            dma((others_core, groups)),
            dma((others_core, groups)),
            dma((1,)),
            dma((others,)),
            dma((others,)),
            dma((groups,)),
            dma((groups,)),
            dma((groups,)),
        ],
        compiler_params=pltpu.CompilerParams(
            collective_id=1, has_side_effects=True, vmem_limit_bytes=48 * 1024 * 1024
        ),
    )(local.reshape(groups, reps, rows, width), stats)


def slots_per_pass(width, refs, atoms):
    share = width * (1.0 - math.exp(-refs / atoms)) + 2.05 * math.sqrt(width)
    return min(-(-width // 16) * 16, -(-int(share) // 16) * 16)


def shards(atom_coords, atom_pairs, traj_ids):
    groups = lax.axis_size("atoms")
    feat_groups = lax.axis_size("feat")
    frames = atom_coords.shape[1]
    frames_here = frames // groups
    part = frames_here // feat_groups
    width = atom_coords.shape[3]
    cols = atom_pairs.shape[1]
    z = lax.axis_index("atoms")
    x = lax.axis_index("feat")

    pairs = lax.all_gather(atom_pairs, "feat", axis=1, tiled=True)
    feats = pairs.shape[1]
    refs = pairs.reshape(-1)
    room = slots_per_pass(width, 2 * feats, width * groups)

    atom_no = jnp.arange(groups * width, dtype=jnp.int32).reshape(groups, width)
    hit = atom_no[:, :, None] == refs[None, None, :]
    used = jnp.any(hit, axis=2)
    before = (jnp.arange(width)[:, None] < jnp.arange(width)[None, :]).astype(jnp.bfloat16)
    rank = matmul(used.astype(jnp.bfloat16), before, ((1,), (0,)))
    most = jnp.max(jnp.sum(used.astype(jnp.float32), 1))
    ref_rank = jnp.sum(jnp.where(hit, rank[:, :, None], 0.0), axis=(0, 1)).reshape(2, feats)
    ref_shard = pairs // width
    used_own = lax.dynamic_index_in_dim(used, z, 0, False)
    rank_own = lax.dynamic_index_in_dim(rank, z, 0, False)

    coords = jnp.transpose(atom_coords[0], (1, 0, 2))
    lanes = 128 if part % 128 == 0 else part
    chunks = part // lanes

    def spots(turn):
        spot = ref_rank - turn * jnp.float32(room)
        inside = (spot >= 0) & (spot < room)
        return jnp.where(inside, ref_shard * room + spot.astype(jnp.int32), -1).T

    def one_pass():
        picked = jnp.where(used_own, rank_own.astype(jnp.int32), -1)[None]
        return exchange(coords, picked, spots(jnp.float32(0.0)), room, lanes, groups, feat_groups)

    def more_passes():
        def step(carry):
            turn, delta = carry
            spot = spots(turn)
            slot = jnp.arange(room, dtype=jnp.float32) + turn * jnp.float32(room)
            pick = ((rank_own[None, :] == slot[:, None]) & used_own[None, :]).astype(jnp.bfloat16)
            grouped = coords.reshape(3, groups, feat_groups, part, width)
            blocks = lax.dynamic_index_in_dim(grouped, x, 2, False)
            chosen = matmul(pick, blocks, ((1,), (3,))).astype(jnp.bfloat16)
            chosen = jnp.transpose(chosen.reshape(room, 3, groups, chunks, lanes), (2, 3, 0, 1, 4))
            chosen = chosen.reshape(groups, chunks, room, 3 * lanes)
            got = lax.all_to_all(chosen, "atoms", split_axis=0, concat_axis=0, tiled=True)
            got = jnp.transpose(got, (0, 2, 1, 3)).reshape(groups * room, chunks * 3 * lanes)
            place = jnp.arange(groups * room, dtype=jnp.int32)
            sign = (spot[:, :1] == place).astype(jnp.bfloat16) - (spot[:, 1:] == place).astype(jnp.bfloat16)
            return turn + 1.0, delta + matmul(sign, got, ((1,), (0,)))

        _, delta = lax.while_loop(
            lambda c: c[0] * room < most,
            step,
            (jnp.float32(0.0), jnp.zeros((feats, chunks * 3 * lanes), jnp.float32)),
        )
        delta = delta.reshape(feats, chunks, 3, lanes)
        computed = jnp.sqrt(jnp.sum(delta * delta, axis=2) + 0.01).reshape(feats, part)
        both = jnp.zeros((feats, frames_here), jnp.float32)
        for o in range(feat_groups):
            turned = lax.ppermute(computed, "feat", [(i, (i + o) % feat_groups) for i in range(feat_groups)])
            both = lax.dynamic_update_slice_in_dim(both, turned, ((x - o) % feat_groups) * part, 1)
        first = lax.dynamic_slice_in_dim(both[:, :HALO], x * cols, cols, 0).T
        return both, lax.ppermute(first, "atoms", [(i, (i - 1) % groups) for i in range(groups)])

    every, incoming = lax.cond(most <= room, one_pass, more_passes)
    every = every.T
    own = lax.dynamic_slice_in_dim(every, x * cols, cols, 1)
    future = jnp.concatenate([own[LAG:], incoming[:LAG]], 0)

    ids = jnp.concatenate([traj_ids[0], jnp.full((LAG,), -1, jnp.int32)])
    ids_now = lax.dynamic_slice_in_dim(ids, z * frames_here, frames_here)
    ids_later = lax.dynamic_slice_in_dim(ids, z * frames_here + LAG, frames_here)
    valid = (ids_now == ids_later).astype(jnp.float32)[:, None]

    count_b = jnp.sum(valid)
    inverse = 1.0 / jnp.maximum(count_b, 1.0)
    now_b = jnp.sum(valid * every, 0) * inverse
    next_b = jnp.sum(valid * future, 0) * inverse
    now_c = valid * (every - now_b)
    next_c = valid * (future - next_b)
    own_c = lax.dynamic_slice_in_dim(now_c, x * cols, cols, 1)
    stats = jnp.concatenate(
        [now_b, next_b, jnp.sum(now_c * now_c, 0), jnp.sum(next_c * next_c, 0), jnp.full((128,), count_b)]
    )
    reps = lax.axis_size("rep")
    stats = jnp.pad(stats, (0, -stats.shape[0] % 1024)).reshape(-1, 128)
    local = matmul(now_c, jnp.concatenate([own_c, next_c], 1), ((0,), (0,)), lax.Precision.HIGH)
    mine, stats = reduce_blocks(local, stats, groups, reps)
    stats = stats.reshape(groups * reps, -1)

    counts = stats[:, 2 * feats + 2 * cols :][:, :1]
    now_all = stats[:, :feats]
    next_all = stats[:, feats : feats + cols]
    sq_now = stats[:, feats + cols : 2 * feats + cols]
    sq_next = stats[:, 2 * feats + cols : 2 * feats + 2 * cols]
    count = jnp.sum(counts)
    mean_now = jnp.sum(counts * now_all, 0) / count
    mean_next = jnp.sum(counts * next_all, 0) / count
    off_now = now_all - mean_now
    off_next = next_all - mean_next
    spread_now = jnp.sum(sq_now + counts * off_now * off_now, 0)
    spread_next = jnp.sum(sq_next + counts * off_next * off_next, 0)
    scale_now = 1.0 / jnp.sqrt(spread_now / count + 1e-05)
    scale_next = 1.0 / jnp.sqrt(spread_next / count + 1e-05)

    rows = feats // lax.axis_size(("atoms", "rep"))
    row = lax.axis_index(("atoms", "rep")) * rows
    off_rows = lax.dynamic_slice_in_dim(off_now, row, rows, 1)
    off_cols = lax.dynamic_slice_in_dim(off_now, x * cols, cols, 1)
    mine = mine + matmul(
        counts * off_rows, jnp.concatenate([off_cols, off_next], 1), ((0,), (0,)), lax.Precision.HIGHEST
    )
    scale_rows = lax.dynamic_slice_in_dim(scale_now, row, rows)
    scale_cols = lax.dynamic_slice_in_dim(scale_now, x * cols, cols)
    mean_cols = lax.dynamic_slice_in_dim(mean_now, x * cols, cols)
    corr_inst = mine[:, :cols] / count * scale_rows[:, None] * scale_cols[None, :]
    corr_lag = mine[:, cols:] / count * scale_rows[:, None] * scale_next[None, :]
    projections = ((own - mean_cols) * scale_cols)[None]
    return (corr_inst, corr_lag, projections)


def solution(mesh):
    placed = (P(("grp", "rep"), None, None, "atoms"), P(None, "feat"), P(("grp", "rep"), None))
    return jax.shard_map(
        shards,
        mesh=mesh,
        in_specs=placed,
        out_specs=(
            P(("grp", "atoms", "rep"), "feat"),
            P(("grp", "atoms", "rep"), "feat"),
            P(("grp", "rep"), "atoms", "feat"),
        ),
        check_vma=False,
    )
```

profile of v0, /device:TPU:0, one launch (start us, length us, event | category | flops | bytes accessed | tf_op | source)
XLA Modules:
  0.0 171.4 jit_solution(3960003075280894566)
XLA Ops:
  0.6 0.8 copy.49
  1.5 9.9 %all_gather.3 = s32[2,1024]{0,1:T(8,128)S(1)} all-gather(s32[2,512]{0,1:T(8,128)S(1)} %copy.49), channel_id=1, replica_groups=mesh['grp'=2,'atoms'=4,'feat'=2,'rep'=2] {'feat'}, dimensions={1}, use_global_device_ids=true | all-gather | bytes 12288 | tf_op jit(solution)/shard_map/all_gather | solution.py:393
  11.4 0.2 copy.50
  11.6 3.7 %compare_reduce_fusion = pred[4,768]{1,0:T(4,128)(4,1)S(1)} fusion(s32[2048]{0:T(1024)S(1)} %bitcast.109, s32[4,768]{1,0:T(4,128)S(1)} %multiply_add_fusion), kind=kLoop, calls=%fused_computation.29 | loop fusion | flops 12579840 | bytes 23552 | tf_op jit(solution)/shard_map/reduce_or | solution.py:400
  15.3 0.2 fusion.24
  15.6 3.0 %fusion.23 = f32[2048]{0:T(1024)S(1)} fusion(f32[4,768]{1,0:T(4,128)S(1)} %fusion.24, s32[2048]{0:T(1024)S(1)} %bitcast.110, s32[4,768]{1,0:T(4,128)S(1)} %multiply_add_fusion), kind=kLoop, calls=%fused_computation.30 | loop fusion | flops 18872320 | bytes 40960 | tf_op jit(solution)/shard_map/reduce_sum | solution.py:404
  18.6 0.1 convert_reduce_fusion
  18.7 0.6 reduce_max.9
  19.3 0.3 add_select_fusion
  20.3 71.1 %conditional.1 = (f32[1024,512]{0,1:T(8,128)}, f32[10,512]{1,0:T(8,128)S(1)}) conditional(s32[]{:T(128)} %convert_element_type.44, (bf16[3,2048,768]{2,1,0:T(8,128)(2,1)}, s32[]{:T(128)}, f32[]{:T(128)}, f32[2,1024]{1,0:T(2,128)S(1)}, s32[2,1024]{0,1:T(8,128)S(1)}, /*index=5*/f32[768]{0:T(1024)S(1)}, pred[768]{0:T(1024)(128)(4,1)S(1)}) %tuple.72, ...), branch_computations={%region_4.8_spmd, %region_8.9_spmd} | conditional | flops 4774863360 | bytes 125673448 | solution.py:453
  20.6 0.2 copy.52
  20.8 0.1 select_bitcast_fusion.slots
  21.0 68.6 %branch_1_fun.1 = (f32[1024,512]{1,0:T(8,128)S(1)}, f32[16,512]{1,0:T(8,128)S(1)}) custom-call(bf16[3,2048,768]{2,1,0:T(8,128)(2,1)} %get-tuple-element.142.coords, s32[1,768]{1,0:T(1,128)S(1)} %broadcast_in_dim.30.picked, s32[1024,2]{1,0:T(8,128)S(1)} %select_bitcast_fusion.slots), custom_call_target="tpu_custom_call" | custom-call | tf_op jit(solution)/shard_map/cond/branch_1_fun/pallas_call | solution.py:194
  89.5 1.9 %copy.48 = f32[1024,512]{0,1:T(8,128)} copy(f32[1024,512]{1,0:T(8,128)S(1)} %get-tuple-element.221) | data formatting | bytes 4194304 | tf_op jit(solution)/shard_map
  91.4 0.7 fusion.49
  92.1 1.8 %multiply_reduce_fusion.1 = f32[1024]{0:T(1024)S(1)} fusion(f32[1024,512]{0,1:T(8,128)} %get-tuple-element.156, f32[512]{0:T(512)S(1)} %get-tuple-element.264), kind=kLoop, calls=%fused_computation.39 | loop fusion | flops 1047552 | bytes 2103296 | tf_op jit(solution)/shard_map/reduce_sum | solution.py:465
  94.6 2.0 %multiply_reduce_fusion = (f32[1024]{0:T(1024)S(1)}, f32[1024,512]{0,1:T(8,128)S(1)}) fusion(f32[1024,512]{0,1:T(8,128)} %get-tuple-element.156, f32[1024]{0:T(1024)S(1)} %get-tuple-element.262, f32[512]{0:T(512)S(1)} %get-tuple-element.264), kind=kLoop, calls=%fused_computation.37 | loop fusion | flops 2096128 | bytes 4204544 | tf_op jit(solution)/shard_map/reduce_sum | solution.py:471
  96.6 1.4 dynamic-slice_bitcast_fusion.2
  98.0 0.1 slice.58
  98.2 0.2 multiply_reduce_fusion.3
  98.3 0.2 multiply_reduce_fusion.2
  98.6 0.6 constant_dynamic-update-slice_fusion.2
  99.2 3.5 %fusion.25 = f32[1024,1024]{1,0:T(8,128)S(1)} fusion(f32[1024,512]{0,1:T(8,128)S(1)} %get-tuple-element.258, f32[512,512]{1,0:T(8,128)S(1)} %get-tuple-element.256, f32[512,512]{1,0:T(8,128)S(1)} %get-tuple-element.272), kind=kOutput, calls=%fused_computation.33 | convolution fusion | flops 3221749760 | bytes 8388608 | tf_op jit(solution)/shard_map/dot_general | solution.py:16
  102.8 60.9 %shard_map.58 = (f32[128,1024]{1,0:T(8,128)S(1)}, f32[8,32,128]{2,1,0:T(8,128)S(1)}) custom-call(f32[4,2,128,1024]{3,2,1,0:T(8,128)S(1)} %bitcast.81, f32[32,128]{1,0:T(8,128)S(1)} %pad_bitcast_fusion.stats), custom_call_target="tpu_custom_call" | custom-call | tf_op jit(solution)/shard_map/pallas_call | solution.py:349
  163.8 0.7 slice_reduce_fusion
  164.6 0.7 broadcast_divide_fusion
  165.4 0.7 add_rsqrt_fusion
  166.3 1.1 multiply_bitcast_fusion
  167.6 0.7 broadcast_divide_fusion.1
  168.3 0.7 add_rsqrt_fusion.1
  169.1 0.7 convolution_add_fusion
  169.8 1.6 fusion.31
  (24 shorter events, 0.9 us)
Async XLA Ops:
  20.3 71.1 %copy-start.2 = (s32[1,2048]{1,0:T(1,128)S(1)}, s32[1,2048]{1,0:T(1,128)}, u32[]{:S(2)}) copy-start(s32[1,2048]{1,0:T(1,128)} %param.9) | copy-start | bytes 24580
where the time goes:
time: 172 us; the launch traced here: 171 us
  Pallas kernels  129 us (75%)
  other arithmetic  19.2 us (11%)
  blocking collectives  9.94 us (6%)
  local copies, waits for them, and re-layouts  5.82 us (3%)
  matrix products  4.46 us (3%)
  between operations  2.19 us (1%)
    pallas_call x1, Pallas kernels, exchange(): pl.pallas_call(functools.partial(exchange_kernel, groups, feat_groups, ro...  68.6 us
    pallas_call x1, Pallas kernels, reduce_blocks(): pl.pallas_call(functools.partial(reduce_kernel, groups, reps), out_shape=...  60.9 us
    all_gather x1, blocking collectives, shards(): pairs = lax.all_gather(atom_pairs, 'feat', axis=1, tiled=True)  9.94 us
    dot_general x3, matrix products, matmul(): lax.dot_general(left, right, (dims, ((), ())), precision=precision, prefe...  4.46 us
    reduce_or x1, other arithmetic, shards(): used = jnp.any(hit, axis=2)  3.68 us

commit v1 on v0

--- a/solution.py
+++ b/solution.py
@@ -10,6 +10,7 @@
 
 LAG = 10
 HALO = 16
+CODE = 32700.0
 
 
 def matmul(left, right, dims, precision=None):
@@ -221,9 +222,38 @@
     )(coords, picked, slots)
 
 
-def reduce_kernel(groups, reps, local, stats, out, gathered, core, sums, left, right, *sems):
+def encode(inst, lag):
+    def one(v):
+        root = v * lax.rsqrt(jnp.abs(v) + 1e-30)
+        return jnp.round(root * CODE).astype(jnp.int32)
+
+    return (one(inst) << 16) | (one(lag) & 0xFFFF)
+
+
+def decode(word):
+    def one(q):
+        root = q.astype(jnp.float32) * (1.0 / CODE)
+        return root * jnp.abs(root)
+
+    return one(word >> 16), one((word << 16) >> 16)
+
+
+def split(value):
+    high = value.astype(jnp.bfloat16)
+    return high, (value - high.astype(jnp.float32)).astype(jnp.bfloat16)
+
+
+def moments_kernel(
+    groups, reps, every, halo, ids, inst, lag, proj, ext, vcol, left3, right3, local, core, stats, gathered,
+    table, side, columns, scales, sums, from_below, from_above, *sems
+):
     c_send, c_recv, s_own, s_send, s_recv, z_send, l_recv, r_recv = sems
-    z, r = lax.axis_index("atoms"), lax.axis_index("rep")
+    z, r, x = lax.axis_index("atoms"), lax.axis_index("rep"), lax.axis_index("feat")
+    frames, feats = every.shape
+    cols = halo.shape[1]
+    rows = inst.shape[0]
+    blocks = groups * reps
+    me = z * reps + r
     peers = [(a, b) for a in range(groups) for b in range(reps) if (a, b) != (0, 0)]
     barrier = pltpu.get_barrier_semaphore()
 
@@ -232,26 +262,70 @@
 
     for a, b in peers:
         pl.semaphore_signal(barrier, 1, device_id=peer(a, b), device_id_type=MESH)
+
+    here = ids[:, pl.ds(pl.multiple_of(z * frames, 128), frames)]
+    after = ids[:, pl.ds(pl.multiple_of(jnp.minimum(z + 1, groups - 1) * frames, 128), 128)]
+    after = jnp.where(z == groups - 1, -1, after)
+    names = jnp.concatenate([here, after], 1).astype(jnp.float32)
+    names = jnp.broadcast_to(names, (8, frames + 128))
+    later = pltpu.roll(names, frames + 128 - LAG, 1)
+    valid = (names == later).astype(jnp.float32)[:, :frames]
+    count = jnp.sum(valid[:1], axis=1, keepdims=True)
+    inverse = 1.0 / jnp.maximum(count, 1.0)
+    vcol[...] = valid.T
+
+    own = pl.ds(pl.multiple_of(x * cols, 128), cols)
+    ext[:frames, :] = every[:, own]
+    ext[frames:, :] = halo[...]
+    step = 32
+
+    def moved(i):
+        wide = ext[pl.ds(pl.multiple_of(i * step, step), step + 16), :]
+        return pltpu.roll(wide, step + 16 - LAG, 0)[:step]
+
+    def fold(value):
+        return jnp.sum(value.reshape(step // 8, 8, value.shape[1]), 0)
+
+    def first(i, carry):
+        at = pl.ds(pl.multiple_of(i * step, step), step)
+        weight = vcol[at, :1]
+        return carry[0] + fold(every[at, :] * weight), carry[1] + fold(moved(i) * weight)
+
+    zero = (jnp.zeros((8, feats), jnp.float32), jnp.zeros((8, cols), jnp.float32))
+    now_sum, next_sum = lax.fori_loop(0, frames // step, first, zero)
+    now_mean = jnp.sum(now_sum, 0, keepdims=True) * inverse
+    next_mean = jnp.sum(next_sum, 0, keepdims=True) * inverse
+
+    def second(i, carry):
+        base = pl.multiple_of(i * step, step)
+        at, at1, at2 = pl.ds(base, step), pl.ds(base + frames, step), pl.ds(base + 2 * frames, step)
+        weight = vcol[at, :1]
+        now = (every[at, :] - now_mean) * weight
+        later = (moved(i) - next_mean) * weight
+        high, low = split(now)
+        left3[at, :] = high
+        left3[at1, :] = high
+        left3[at2, :] = low
+        right3[at, :cols] = left3[at, own]
+        right3[at1, :cols] = left3[at2, own]
+        right3[at2, :cols] = left3[at, own]
+        high, low = split(later)
+        right3[at, cols:] = high
+        right3[at1, cols:] = low
+        right3[at2, cols:] = high
+        return carry[0] + fold(now * now), carry[1] + fold(later * later)
+
+    now_sq, next_sq = lax.fori_loop(0, frames // step, second, zero)
+    stats[...] = jnp.zeros_like(stats)
+    stats[0:1, :] = now_mean
+    stats[1:2, :] = jnp.sum(now_sq, 0, keepdims=True)
+    stats[2:3, :cols] = next_mean
+    stats[3:4, :cols] = jnp.sum(next_sq, 0, keepdims=True)
+    stats[4:5, :] = jnp.broadcast_to(count, (1, feats))
     pl.semaphore_wait(barrier, len(peers))
 
-    order = []
-    for k in range((groups + 1) // 2):
-        order += [groups - 1 - k] + ([k] if k != groups - 1 - k else [])
-    core_copies = {}
-    for d in order:
-        for b in range(1, reps):
-            core_copies[d, b] = pltpu.make_async_remote_copy(
-                src_ref=local.at[d, lax.rem(r + b, reps)],
-                dst_ref=core.at[b - 1, d],
-                send_sem=c_send.at[b - 1, d],
-                recv_sem=c_recv.at[b - 1, d],
-                device_id={"rep": lax.rem(r + b, reps)},
-                device_id_type=MESH,
-            )
-            core_copies[d, b].start()
-    me = z * reps + r
-    own = pltpu.make_async_copy(stats, gathered.at[me], s_own.at[0])
-    own.start()
+    own_stats = pltpu.make_async_copy(stats, gathered.at[me], s_own.at[0])
+    own_stats.start()
     stat_copies = []
     for k, (a, b) in enumerate(peers):
         stat_copies.append(
@@ -266,99 +340,246 @@
         )
         stat_copies[-1].start()
 
-
-    def hop(d, step):
+    def core_copy(d, b):
+        return pltpu.make_async_remote_copy(
+            src_ref=local.at[d, lax.rem(r + b, reps)],
+            dst_ref=core.at[b - 1, d],
+            send_sem=c_send.at[b - 1, d],
+            recv_sem=c_recv.at[b - 1, d],
+            device_id={"rep": lax.rem(r + b, reps)},
+            device_id_type=MESH,
+        )
+
+    tile = max(128, reps * rows)
+    tiles, inside = feats // tile, tile // (reps * rows)
+
+    def product(k, carry):
+        half = k // 2
+        t = jnp.where(k % 2 == 0, tiles - 1 - half, half)
+        at = pl.ds(pl.multiple_of(t * tile, tile), tile)
+        got = lax.dot_general(
+            left3[:, at], right3[...], (((0,), (0,)), ((), ())), preferred_element_type=jnp.float32
+        )
+        for j in range(inside):
+            d = t * inside + j
+            for b in range(reps):
+                low = (j * reps + b) * rows
+                local[d, b] = got[low : low + rows]
+            for b in range(1, reps):
+                core_copy(d, b).start()
+        return carry
+
+    lax.fori_loop(0, tiles, product, 0)
+
+    own_stats.wait()
+    for copy in stat_copies:
+        copy.wait()
+
+    total = jnp.zeros((1, feats), jnp.float32)
+    now_total = jnp.zeros((1, feats), jnp.float32)
+    next_total = jnp.zeros((1, cols), jnp.float32)
+    for b in range(blocks):
+        size = gathered[b, 4:5, :]
+        total = total + size
+        now_total = now_total + size * gathered[b, 0:1, :]
+        next_total = next_total + size[:, :cols] * gathered[b, 2:3, :cols]
+    mean_now = now_total / total
+    mean_next = next_total / total[:, :cols]
+    now_spread = jnp.zeros((1, feats), jnp.float32)
+    next_spread = jnp.zeros((1, cols), jnp.float32)
+    for b in range(blocks):
+        size = gathered[b, 4:5, :]
+        off = gathered[b, 0:1, :] - mean_now
+        now_spread = now_spread + (gathered[b, 1:2, :] + size * off * off)
+        off = gathered[b, 2:3, :cols] - mean_next
+        next_spread = next_spread + (gathered[b, 3:4, :cols] + size[:, :cols] * off * off)
+    scale_now = 1.0 / jnp.sqrt(now_spread / total + 1e-05)
+    scale_next = 1.0 / jnp.sqrt(next_spread / total[:, :cols] + 1e-05)
+    root = 1.0 / jnp.sqrt(total)
+    table[blocks : blocks + 1, :] = scale_now * root
+    table[blocks + 1 : blocks + 2, :] = mean_now
+    table[blocks + 2 : blocks + 3, :] = scale_now
+    table[blocks + 3 :, :] = jnp.zeros((5, feats), jnp.float32)
+    for b in range(blocks):
+        size = gathered[b, 4:5, :]
+        table[b : b + 1, :] = (gathered[b, 0:1, :] - mean_now) * (scale_now * root)
+        side[b : b + 1, cols:] = (
+            size[:, :cols] * (gathered[b, 2:3, :cols] - mean_next) * (scale_next * root[:, :cols])
+        )
+    for b in range(blocks):
+        side[b : b + 1, :cols] = gathered[b, 4:5, :cols] * table[b : b + 1, own]
+    scales[0:1, :cols] = table[blocks : blocks + 1, own]
+    scales[0:1, cols:] = scale_next * root[:, :cols]
+    columns[...] = table[...].T
+
+    tall = min(rows, 32)
+
+    def hop(d, up):
         return pltpu.make_async_remote_copy(
             src_ref=sums.at[d],
-            dst_ref=(left if step > 0 else right).at[d],
+            dst_ref=(from_below if up else from_above).at[d],
             send_sem=z_send.at[d],
-            recv_sem=(l_recv if step > 0 else r_recv).at[d],
-            device_id={"atoms": lax.rem(z + step + groups, groups)},
+            recv_sem=(l_recv if up else r_recv).at[d],
+            device_id={"atoms": lax.rem(z + (1 if up else groups - 1), groups)},
             device_id_type=MESH,
         )
 
-    for d in order:
-        total = local[d, r]
+    def mine(d, i):
+        at = pl.ds(pl.multiple_of(i * tall, tall), tall)
+        value = local[d, r, at, :]
         for b in range(1, reps):
-            core_copies[d, b].wait_recv()
-            total = total + core[b - 1, d]
-        sums[d] = total
-
-        if d > 0:
+            value = value + core[b - 1, d, at, :]
+        high = pl.ds(pl.multiple_of((d * reps + r) * rows + i * tall, tall), tall)
+        return value * columns[high, blocks : blocks + 1] * scales[0:1, :]
+
+    def wait_core(d):
+        for b in range(1, reps):
+            core_copy(d, b).wait_recv()
+
+    def send(d, up, relay):
+        if relay:
+            hop(d, up).wait_recv()
+
+        def body(i, carry):
+            at = pl.ds(pl.multiple_of(i * tall, tall), tall)
+            value = mine(d, i)
+            inst_part, lag_part = value[:, :cols], value[:, cols:]
+            if relay:
+                more = decode((from_below if up else from_above)[d, at, :])
+                inst_part, lag_part = inst_part + more[0], lag_part + more[1]
+            sums[d, at, :] = encode(inst_part, lag_part)
+            return carry
+
+        lax.fori_loop(0, rows // tall, body, 0)
+        hop(d, up).start()
+
+    def chain(k, carry):
+        above, below = groups - 1 - k, k
+
+        @pl.when(z < above)
+        def _():
+            wait_core(above)
 
             @pl.when(z == 0)
-            def _(d=d):
-                hop(d, 1).start()
-
-        if d < groups - 1:
+            def _():
+                send(above, True, False)
+
+            @pl.when(z > 0)
+            def _():
+                send(above, True, True)
+
+        @pl.when(z > below)
+        def _():
+            wait_core(below)
 
             @pl.when(z == groups - 1)
-            def _(d=d):
-                hop(d, -1).start()
-
-    for k in range(groups):
-        up, down = groups - 1 - k, k
-
-        @pl.when((z > 0) & (z < up))
-        def _(d=up):
-            hop(d, 1).wait_recv()
-            sums[d] = sums[d] + left[d]
-            hop(d, 1).start()
-
-        @pl.when((z < groups - 1) & (z > down))
-        def _(d=down):
-            hop(d, -1).wait_recv()
-            sums[d] = sums[d] + right[d]
-            hop(d, -1).start()
-
-    for d in range(groups):
-
-        @pl.when(z == d)
-        def _(d=d):
-            total = sums[d]
-            if d > 0:
-                hop(d, 1).wait_recv()
-                total = total + left[d]
-            if d < groups - 1:
-                hop(d, -1).wait_recv()
-                total = total + right[d]
-            out[...] = total
+            def _():
+                send(below, False, False)
+
+            @pl.when(z < groups - 1)
+            def _():
+                send(below, False, True)
+
+        return carry
+
+    lax.fori_loop(0, groups, chain, 0)
+
+    wait_core(z)
+
+    def settle(i, carry):
+        at = pl.ds(pl.multiple_of(i * tall, tall), tall)
+        high = pl.ds(pl.multiple_of(me * rows + i * tall, tall), tall)
+        shift = lax.dot_general(
+            columns[high, :blocks], side[...], (((1,), (0,)), ((), ())),
+            precision=lax.Precision.HIGHEST, preferred_element_type=jnp.float32,
+        )
+        value = mine(z, i) + shift
+        inst[at, :] = value[:, :cols]
+        lag[at, :] = value[:, cols:]
+        return carry
+
+    lax.fori_loop(0, rows // tall, settle, 0)
+
+    center, stretch = table[blocks + 1 : blocks + 2, own], table[blocks + 2 : blocks + 3, own]
+
+    def project(i, carry):
+        at = pl.ds(pl.multiple_of(i * step, step), step)
+        proj[at, :] = (ext[at, :] - center) * stretch
+        return carry
+
+    lax.fori_loop(0, frames // step, project, 0)
+
+    def arrive(up):
+        hop(z, up).wait_recv()
+
+        def body(i, carry):
+            at = pl.ds(pl.multiple_of(i * tall, tall), tall)
+            more = decode((from_below if up else from_above)[z, at, :])
+            inst[at, :] = inst[at, :] + more[0]
+            lag[at, :] = lag[at, :] + more[1]
+            return carry
+
+        lax.fori_loop(0, rows // tall, body, 0)
+
+    @pl.when(z > 0)
+    def _():
+        arrive(True)
+
+    @pl.when(z < groups - 1)
+    def _():
+        arrive(False)
+
+    def finish(d, carry):
+        for b in range(1, reps):
+            core_copy(d, b).wait_send()
 
         @pl.when(z < d)
-        def _(d=d):
-            hop(d, 1).wait_send()
+        def _():
+            hop(d, True).wait_send()
 
         @pl.when(z > d)
-        def _(d=d):
-            hop(d, -1).wait_send()
-
-    for copy in core_copies.values():
-        copy.wait_send()
-    own.wait()
-    for copy in stat_copies:
-        copy.wait()
-
-
-def reduce_blocks(local, stats, groups, reps):
-    rows, width = local.shape[0] // (groups * reps), local.shape[1]
+        def _():
+            hop(d, False).wait_send()
+
+        return carry
+
+    lax.fori_loop(0, groups, finish, 0)
+
+
+def moments(every, halo, ids, groups, reps):
+    frames, feats = every.shape
+    cols = halo.shape[1]
+    blocks = groups * reps
+    rows = feats // blocks
     vmem = pl.BlockSpec(memory_space=pltpu.VMEM)
     dma = pltpu.SemaphoreType.DMA
-    block = pltpu.VMEM((groups, rows, width), jnp.float32)
-    others = max(groups * reps - 1, 1)
-    others_core = max(reps - 1, 1)
+    others, others_core = max(blocks - 1, 1), max(reps - 1, 1)
+    word = pltpu.VMEM((groups, rows, cols), jnp.int32)
     return pl.pallas_call(
-        functools.partial(reduce_kernel, groups, reps),
+        functools.partial(moments_kernel, groups, reps),
         out_shape=(
-            jax.ShapeDtypeStruct((rows, width), jnp.float32),
-            jax.ShapeDtypeStruct((groups * reps,) + stats.shape, jnp.float32),
+            jax.ShapeDtypeStruct((rows, cols), jnp.float32),
+            jax.ShapeDtypeStruct((rows, cols), jnp.float32),
+            jax.ShapeDtypeStruct((frames, cols), jnp.float32),
         ),
-        in_specs=[vmem, vmem],
-        out_specs=(vmem, vmem),
+        in_specs=[vmem, vmem, vmem],
+        out_specs=(vmem, vmem, vmem),
         scratch_shapes=[
-            pltpu.VMEM((others_core, groups, rows, width), jnp.float32),
-            block,
-            block,
-            block,
+            pltpu.VMEM((frames + HALO, cols), jnp.float32),
+            pltpu.VMEM((frames, 8), jnp.float32),
+            pltpu.VMEM((3 * frames, feats), jnp.bfloat16),
+            pltpu.VMEM((3 * frames, 2 * cols), jnp.bfloat16),
+            pltpu.VMEM((groups, reps, rows, 2 * cols), jnp.float32),
+            pltpu.VMEM((others_core, groups, rows, 2 * cols), jnp.float32),
+            pltpu.VMEM((8, feats), jnp.float32),
+            pltpu.VMEM((blocks, 8, feats), jnp.float32),
+            pltpu.VMEM((blocks + 8, feats), jnp.float32),
+            pltpu.VMEM((blocks, 2 * cols), jnp.float32),
+            pltpu.VMEM((feats, blocks + 8), jnp.float32),
+            pltpu.VMEM((8, 2 * cols), jnp.float32),
+            word,
+            word,
+            word,
             dma((others_core, groups)),
             dma((others_core, groups)),
             dma((1,)),
@@ -369,9 +590,9 @@
             dma((groups,)),
         ],
         compiler_params=pltpu.CompilerParams(
-            collective_id=1, has_side_effects=True, vmem_limit_bytes=48 * 1024 * 1024
+            collective_id=1, has_side_effects=True, vmem_limit_bytes=56 * 1024 * 1024
         ),
-    )(local.reshape(groups, reps, rows, width), stats)
+    )(every, halo, ids)
 
 
 def slots_per_pass(width, refs, atoms):
@@ -451,60 +672,8 @@
         return both, lax.ppermute(first, "atoms", [(i, (i - 1) % groups) for i in range(groups)])
 
     every, incoming = lax.cond(most <= room, one_pass, more_passes)
-    every = every.T
-    own = lax.dynamic_slice_in_dim(every, x * cols, cols, 1)
-    future = jnp.concatenate([own[LAG:], incoming[:LAG]], 0)
-
-    ids = jnp.concatenate([traj_ids[0], jnp.full((LAG,), -1, jnp.int32)])
-    ids_now = lax.dynamic_slice_in_dim(ids, z * frames_here, frames_here)
-    ids_later = lax.dynamic_slice_in_dim(ids, z * frames_here + LAG, frames_here)
-    valid = (ids_now == ids_later).astype(jnp.float32)[:, None]
-
-    count_b = jnp.sum(valid)
-    inverse = 1.0 / jnp.maximum(count_b, 1.0)
-    now_b = jnp.sum(valid * every, 0) * inverse
-    next_b = jnp.sum(valid * future, 0) * inverse
-    now_c = valid * (every - now_b)
-    next_c = valid * (future - next_b)
-    own_c = lax.dynamic_slice_in_dim(now_c, x * cols, cols, 1)
-    stats = jnp.concatenate(
-        [now_b, next_b, jnp.sum(now_c * now_c, 0), jnp.sum(next_c * next_c, 0), jnp.full((128,), count_b)]
-    )
-    reps = lax.axis_size("rep")
-    stats = jnp.pad(stats, (0, -stats.shape[0] % 1024)).reshape(-1, 128)
-    local = matmul(now_c, jnp.concatenate([own_c, next_c], 1), ((0,), (0,)), lax.Precision.HIGH)
-    mine, stats = reduce_blocks(local, stats, groups, reps)
-    stats = stats.reshape(groups * reps, -1)
-
-    counts = stats[:, 2 * feats + 2 * cols :][:, :1]
-    now_all = stats[:, :feats]
-    next_all = stats[:, feats : feats + cols]
-    sq_now = stats[:, feats + cols : 2 * feats + cols]
-    sq_next = stats[:, 2 * feats + cols : 2 * feats + 2 * cols]
-    count = jnp.sum(counts)
-    mean_now = jnp.sum(counts * now_all, 0) / count
-    mean_next = jnp.sum(counts * next_all, 0) / count
-    off_now = now_all - mean_now
-    off_next = next_all - mean_next
-    spread_now = jnp.sum(sq_now + counts * off_now * off_now, 0)
-    spread_next = jnp.sum(sq_next + counts * off_next * off_next, 0)
-    scale_now = 1.0 / jnp.sqrt(spread_now / count + 1e-05)
-    scale_next = 1.0 / jnp.sqrt(spread_next / count + 1e-05)
-
-    rows = feats // lax.axis_size(("atoms", "rep"))
-    row = lax.axis_index(("atoms", "rep")) * rows
-    off_rows = lax.dynamic_slice_in_dim(off_now, row, rows, 1)
-    off_cols = lax.dynamic_slice_in_dim(off_now, x * cols, cols, 1)
-    mine = mine + matmul(
-        counts * off_rows, jnp.concatenate([off_cols, off_next], 1), ((0,), (0,)), lax.Precision.HIGHEST
-    )
-    scale_rows = lax.dynamic_slice_in_dim(scale_now, row, rows)
-    scale_cols = lax.dynamic_slice_in_dim(scale_now, x * cols, cols)
-    mean_cols = lax.dynamic_slice_in_dim(mean_now, x * cols, cols)
-    corr_inst = mine[:, :cols] / count * scale_rows[:, None] * scale_cols[None, :]
-    corr_lag = mine[:, cols:] / count * scale_rows[:, None] * scale_next[None, :]
-    projections = ((own - mean_cols) * scale_cols)[None]
-    return (corr_inst, corr_lag, projections)
+    corr_inst, corr_lag, projections = moments(every.T, incoming, traj_ids, groups, lax.axis_size("rep"))
+    return (corr_inst, corr_lag, projections[None])
 
 
 def solution(mesh):

time: 172 us -> 147 us (0.85)
  other arithmetic: 19.2 us -> 7.88 us
  Pallas kernels: 129 us -> 118 us
  matrix products: 4.46 us -> 0.22 us
  local copies, waits for them, and re-layouts: 5.82 us -> 8.79 us
    pallas_call x1, Pallas kernels: 60.9 us -> 49.4 us  [moments(): pl.pallas_call(functools.partial(moments_kernel, groups, reps), out_shape...]
    reduce_sum x10 -> x0, other arithmetic: 5.84 us -> none  [the longest x1 1.96 us: shards(): jnp.sum(now_c * now_c, 0)]
    unnamed x8 -> x5, local copies, waits for them, and re-layouts: 1.01 us -> 6.43 us
    dot_general x3 -> x1, matrix products: 4.46 us -> 0.22 us  [matmul(): lax.dot_general(left, right, (dims, ((), ())), precision=precision, prefe...]
    another operation x2 -> x1, local copies, waits for them, and re-layouts: 2.1 us -> 0.22 us
    pallas_call x0 -> x1, local copies, waits for them, and re-layouts: none -> 1.88 us  [exchange(): pl.pallas_call(functools.partial(exchange_kernel, groups, feat_groups, ro...]
where the time goes in v1:
time: 147 us; the launch traced here: 146 us
  Pallas kernels  118 us (80%)
  blocking collectives  9.94 us (7%)
  local copies, waits for them, and re-layouts  8.79 us (6%)
  other arithmetic  7.88 us (5%)
    pallas_call x1, Pallas kernels, exchange(): pl.pallas_call(functools.partial(exchange_kernel, groups, feat_groups, ro...  68.6 us
    pallas_call x1, Pallas kernels, moments(): pl.pallas_call(functools.partial(moments_kernel, groups, reps), out_shape...  49.4 us
    all_gather x1, blocking collectives, shards(): pairs = lax.all_gather(atom_pairs, 'feat', axis=1, tiled=True)  9.94 us
    unnamed x5, local copies, waits for them, and re-layouts  6.43 us
    reduce_or x1, other arithmetic, shards(): used = jnp.any(hit, axis=2)  3.68 us
    reduce_sum x1, other arithmetic, shards(): jnp.sum(jnp.where(hit, rank[:, :, None], 0.0), axis=(0, 1))  2.98 us

profile of v1, /device:TPU:0, one launch (start us, length us, event | category | flops | bytes accessed | tf_op | source)
XLA Modules:
  0.0 146.4 jit_solution(5620468237547373452)
XLA Ops:
  0.6 0.8 copy.42
  1.5 9.9 %all_gather.3 = s32[2,1024]{0,1:T(8,128)S(1)} all-gather(s32[2,512]{0,1:T(8,128)S(1)} %copy.42), channel_id=1, replica_groups=mesh['grp'=2,'atoms'=4,'feat'=2,'rep'=2] {'feat'}, dimensions={1}, use_global_device_ids=true | all-gather | bytes 12288 | tf_op jit(solution)/shard_map/all_gather | solution.py:614
  11.4 0.2 copy.43
  11.6 3.7 %compare_reduce_fusion = pred[4,768]{1,0:T(4,128)(4,1)S(1)} fusion(s32[2048]{0:T(1024)S(1)} %bitcast.79, s32[4,768]{1,0:T(4,128)S(1)} %multiply_add_fusion), kind=kLoop, calls=%fused_computation.29 | loop fusion | flops 12579840 | bytes 23552 | tf_op jit(solution)/shard_map/reduce_or | solution.py:621
  15.3 0.2 fusion.24
  15.6 3.0 %fusion.23 = f32[2048]{0:T(1024)S(1)} fusion(f32[4,768]{1,0:T(4,128)S(1)} %fusion.24, s32[2048]{0:T(1024)S(1)} %bitcast.80, s32[4,768]{1,0:T(4,128)S(1)} %multiply_add_fusion), kind=kLoop, calls=%fused_computation.30 | loop fusion | flops 18872320 | bytes 40960 | tf_op jit(solution)/shard_map/reduce_sum | solution.py:625
  18.6 0.1 convert_reduce_fusion
  18.7 0.6 reduce_max.9
  19.3 0.3 add_select_fusion
  20.3 71.1 %conditional.1 = (f32[1024,512]{0,1:T(8,128)}, f32[16,512]{1,0:T(8,128)S(1)}) conditional(s32[]{:T(128)} %convert_element_type.38, (bf16[3,2048,768]{2,1,0:T(8,128)(2,1)}, s32[]{:T(128)}, f32[]{:T(128)}, f32[2,1024]{1,0:T(2,128)S(1)}, s32[2,1024]{0,1:T(8,128)S(1)}, /*index=5*/f32[768]{0:T(1024)S(1)}, pred[768]{0:T(1024)(128)(4,1)S(1)}) %tuple.61, ...), branch_computations={%region_4.8_spmd, %region_8.9_spmd} | conditional | flops 4774863360 | bytes 125673448 | solution.py:674
  20.5 0.2 copy.45
  20.8 0.1 select_bitcast_fusion.slots
  20.9 68.6 %branch_1_fun.1 = (f32[1024,512]{1,0:T(8,128)S(1)}, f32[16,512]{1,0:T(8,128)S(1)}) custom-call(bf16[3,2048,768]{2,1,0:T(8,128)(2,1)} %get-tuple-element.139.coords, s32[1,768]{1,0:T(1,128)S(1)} %broadcast_in_dim.29.picked, s32[1024,2]{1,0:T(8,128)S(1)} %select_bitcast_fusion.slots), custom_call_target="tpu_custom_call" | custom-call | tf_op jit(solution)/shard_map/cond/branch_1_fun/pallas_call | solution.py:195
  89.5 1.9 %copy.41 = f32[1024,512]{0,1:T(8,128)} copy(f32[1024,512]{1,0:T(8,128)S(1)} %get-tuple-element.218) | data formatting | bytes 4194304 | tf_op jit(solution)/shard_map/cond/branch_1_fun/pallas_call | solution.py:195
  91.4 49.4 %shard_map.58 = (f32[128,512]{1,0:T(8,128)}, f32[128,512]{1,0:T(8,128)}, f32[512,512]{1,0:T(8,128)}) custom-call(f32[512,1024]{1,0:T(8,128)} %bitcast.18.every, f32[16,512]{1,0:T(8,128)S(1)} %get-tuple-element.153.halo, s32[1,2048]{1,0:T(1,128)} %ids.1), custom_call_target="tpu_custom_call" | custom-call | tf_op jit(solution)/shard_map/pallas_call | solution.py:558
  140.8 1.7 %copy.74 = f32[128,512]{1,0:T(8,128)} copy(f32[128,512]{1,0:T(8,128)} %get-tuple-element.341) | data formatting | bytes 524288
  142.5 1.7 %copy.75 = f32[128,512]{1,0:T(8,128)} copy(f32[128,512]{1,0:T(8,128)} %get-tuple-element.342) | data formatting | bytes 524288
  144.2 2.3 %copy.76 = f32[1,512,512]{2,1,0:T(8,128)} copy(f32[1,512,512]{2,1,0:T(8,128)} %bitcast.75) | data formatting | bytes 2097152
  (7 shorter events, 0.1 us)

commit v2 on v1

--- a/solution.py
+++ b/solution.py
@@ -21,17 +21,19 @@
 MESH = pl.DeviceIdType.MESH
 
 
-def exchange_kernel(
-    groups, feat_groups, room, lanes, chunks, tile, coords, picked, slots, out, halo, *scratch
-):
-    blocks, pick, chosen, sign, recv, edge, load, z_send, z_recv, z_own, x_send, x_recv, h_send, h_recv = scratch
+def exchange_kernel(groups, feat_groups, room, chunks, coords, pairs, every, halo, over, *scratch):
+    (
+        blocks, everyone, ranks, pick, front, back, sign, front_in, back_in, third,
+        load, p_send, p_recv, f_send, f_recv, b_send, b_recv, f_own, b_own, x_send, x_recv, h_send, h_recv,
+    ) = scratch
     z, x = lax.axis_index("atoms"), lax.axis_index("feat")
+    lanes, part = 128, 64
+    width = coords.shape[2]
+    feats, cols = every.shape[1], pairs.shape[1]
     half = groups // 2
     z_steps = [half] + [o for o in range(groups - 1, 0, -1) if o != half] if groups > 1 else []
     x_steps = list(range(1, feat_groups))
-    tiles = out.shape[0] // tile
     frames_here = feat_groups * chunks * lanes
-    cols = halo.shape[1]
     z_dests = [lax.rem(z + o, groups) for o in z_steps] + [z]
     loads = []
     for ch in range(chunks):
@@ -59,9 +61,7 @@
     def _():
         pl.semaphore_signal(barrier, 1, device_id={"atoms": z_up, "feat": 0}, device_id_type=MESH)
 
-    width = picked.shape[1]
-    slot_no = lax.broadcasted_iota(jnp.int32, (room, width), 0)
-    pick[...] = jnp.where(slot_no == picked[...], 1.0, 0.0).astype(jnp.bfloat16)
+    everyone[x] = pairs[...]
 
     @pl.when(x == 0)
     def _():
@@ -71,68 +71,142 @@
     def _():
         pl.semaphore_wait(barrier, len(z_steps) + len(x_steps) + 1)
 
+    pair_copies = []
+    for k, o in enumerate(x_steps):
+        pair_copies.append(
+            pltpu.make_async_remote_copy(
+                src_ref=pairs,
+                dst_ref=everyone.at[x],
+                send_sem=p_send.at[k],
+                recv_sem=p_recv.at[k],
+                device_id={"feat": lax.rem(x + o, feat_groups)},
+                device_id_type=MESH,
+            )
+        )
+        pair_copies[-1].start()
+    for copy in pair_copies:
+        copy.wait()
+
+    lines = -(-width // lanes)
+    height = -(-groups * lines // 16) * 16
+
+    def iota(shape, dim):
+        return lax.broadcasted_iota(jnp.int32, shape, dim)
+
+    def bins(value, size):
+        return sum(((value >= s * size).astype(jnp.int32) for s in range(1, groups)), jnp.zeros_like(value))
+
+    def ones(mask):
+        return jnp.where(mask, 1.0, 0.0).astype(jnp.bfloat16)
+
+    def product(a, b, dims):
+        return lax.dot_general(a, b, (dims, ((), ())), preferred_element_type=jnp.float32)
+
+    found, counts = [], jnp.zeros((height, lanes), jnp.float32)
+    for k in range(2):
+        ref = jnp.concatenate([everyone[i, k : k + 1, :] for i in range(feat_groups)], 1)
+        shard = bins(ref, width)
+        inner = ref - shard * width
+        line = ones(iota((height, feats), 0) == shard * lines + (inner >> 7))
+        spot = ones(iota((lanes, feats), 0) == (inner & 127))
+        counts = counts + product(line, spot, ((1,), (1,)))
+        found.append((shard, line, spot))
+    used = ones(counts > 0.5)
+    earlier = ones(iota((lanes, lanes), 0) < iota((lanes, lanes), 1))
+    row_shard, col_shard = bins(iota((height, height), 0), lines), bins(iota((height, height), 1), lines)
+    same = row_shard == col_shard
+    filled = product(used, jnp.ones((lanes, lanes), jnp.bfloat16), ((1,), (0,))).astype(jnp.bfloat16)
+    before = product(
+        ones(same & (iota((height, height), 1) < iota((height, height), 0))), filled, ((1,), (0,))
+    )
+    rank = product(used, earlier, ((1,), (0,))) + before
+    most = jnp.max(product(ones(same), filled, ((1,), (0,))))
+    over[...] = jnp.where(jnp.broadcast_to(most, over.shape) > room, 1.0, 0.0)
+    ranks[...] = jnp.where(counts > 0.5, rank, -1.0)
+    whole = rank.astype(jnp.int32)
+    parts = jnp.concatenate(
+        [(whole >> 4).astype(jnp.float32), (whole & 15).astype(jnp.float32)], 0
+    ).astype(jnp.bfloat16)
+    slots = []
+    for shard, line, spot in found:
+        got = product(parts, spot, ((1,), (0,)))
+        chosen = (got[:height] * 16.0 + got[height:]) * line.astype(jnp.float32)
+        place = jnp.sum(chosen, 0, keepdims=True).astype(jnp.int32)
+        slots.append(jnp.where(place < room, shard * room + place, -1))
+
+    slot_no = iota((room, lanes), 0).astype(jnp.float32)
+    for j in range(lines):
+        wide = min(lanes, width - j * lanes)
+        row = ranks[pl.ds(z * lines + j, 1), :]
+        pick[:, j * lanes : j * lanes + wide] = ones(slot_no == row)[:, :wide]
+
     def fill(ch, i):
         loads[ch][i].wait()
-        for c in range(3):
-            got = lax.dot_general(
-                pick[...], blocks[ch, i, c], (((1,), (1,)), ((), ())), preferred_element_type=jnp.float32
-            )
-            chosen[ch, i, :, c * lanes : (c + 1) * lanes] = got.astype(jnp.bfloat16)
+
+        def get(first):
+            return product(pick[...], first, ((1,), (1,))).astype(jnp.bfloat16)
+
+        early = [blocks[ch, i, c, :part] for c in range(2)]
+        late = [blocks[ch, i, c, part:] for c in range(2)]
+        front[ch, i, :, :lanes] = get(jnp.concatenate(early, 0))
+        front[ch, i, :, lanes:] = get(blocks[ch, i, 2])
+        back[ch, i] = get(jnp.concatenate(late, 0))
 
     here = pl.ds(pl.multiple_of(z * room, 16), room)
-    z_copies = []
+
+    def z_copy(source, target, send, recv, ch, i):
+        return pltpu.make_async_remote_copy(
+            src_ref=source.at[ch, i],
+            dst_ref=target.at[ch, here],
+            send_sem=send.at[ch, i],
+            recv_sem=recv.at[ch, i],
+            device_id={"atoms": z_dests[i]},
+            device_id_type=MESH,
+        )
+
+    fronts, backs = [], []
     for ch in range(chunks):
-        row = []
-        for i, o in enumerate(z_steps):
+        fronts.append([])
+        backs.append([])
+        for i in range(len(z_steps)):
             fill(ch, i)
-            row.append(
-                pltpu.make_async_remote_copy(
-                    src_ref=chosen.at[ch, i],
-                    dst_ref=recv.at[ch, here],
-                    send_sem=z_send.at[ch, i],
-                    recv_sem=z_recv.at[ch, i],
-                    device_id={"atoms": z_dests[i]},
-                    device_id_type=MESH,
-                )
-            )
-            row[-1].start()
-        z_copies.append(row)
-    own_copies = []
+            fronts[ch].append(z_copy(front, front_in, f_send, f_recv, ch, i))
+            fronts[ch][i].start()
+        for i in range(len(z_steps)):
+            backs[ch].append(z_copy(back, back_in, b_send, b_recv, ch, i))
+            backs[ch][i].start()
+    last = len(z_steps)
+    front_own, back_own = [], []
     for ch in range(chunks):
-        fill(ch, len(z_steps))
-        own_copies.append(
-            pltpu.make_async_copy(chosen.at[ch, len(z_steps)], recv.at[ch, here], z_own.at[ch])
-        )
-        own_copies[-1].start()
-
-    place = lax.broadcasted_iota(jnp.int32, (128, groups * room), 1)
+        fill(ch, last)
+        front_own.append(pltpu.make_async_copy(front.at[ch, last], front_in.at[ch, here], f_own.at[ch]))
+        back_own.append(pltpu.make_async_copy(back.at[ch, last], back_in.at[ch, here], b_own.at[ch]))
+        front_own[ch].start()
+        back_own[ch].start()
 
     def make_sign(i, carry):
-        rows = pl.ds(pl.multiple_of(i * 128, 128), 128)
-        pair = slots[rows, :]
-        value = jnp.where(place == pair[:, 0:1], 1.0, 0.0) - jnp.where(place == pair[:, 1:2], 1.0, 0.0)
-        sign[rows, :] = value.astype(jnp.bfloat16)
+        at = pl.ds(pl.multiple_of(i * 16, 16), 16)
+        number = iota((16, feats), 0) + i * 16
+        value = jnp.where(number == slots[0], 1.0, 0.0) - jnp.where(number == slots[1], 1.0, 0.0)
+        sign[at, :] = value.astype(jnp.bfloat16)
         return carry
 
-    lax.fori_loop(0, out.shape[0] // 128, make_sign, 0)
-
-    def x_copy(ch, i, k, o):
-        part = out.at[
-            pl.ds(pl.multiple_of(i * tile, tile), tile),
-            pl.ds(pl.multiple_of((x * chunks + ch) * lanes, lanes), lanes),
-        ]
+    lax.fori_loop(0, groups * room // 16, make_sign, 0)
+
+    def x_copy(ch, p, k, o):
+        at = every.at[pl.ds(pl.multiple_of((x * chunks + ch) * lanes + p * part, part), part), :]
         return pltpu.make_async_remote_copy(
-            src_ref=part,
-            dst_ref=part,
-            send_sem=x_send.at[ch, i, k],
-            recv_sem=x_recv.at[ch, i, k],
+            src_ref=at,
+            dst_ref=at,
+            send_sem=x_send.at[ch, p, k],
+            recv_sem=x_recv.at[ch, p, k],
             device_id={"feat": lax.rem(x + o, feat_groups)},
             device_id_type=MESH,
         )
 
     def h_copy(k):
         return pltpu.make_async_remote_copy(
-            src_ref=edge.at[:, k * cols : (k + 1) * cols],
+            src_ref=every.at[:HALO, k * cols : (k + 1) * cols],
             dst_ref=halo,
             send_sem=h_send.at[k],
             recv_sem=h_recv.at[0],
@@ -140,32 +214,33 @@
             device_id_type=MESH,
         )
 
+    def keep(ch, p, total):
+        at = pl.ds(pl.multiple_of((x * chunks + ch) * lanes + p * part, part), part)
+        every[at, :] = jnp.sqrt(total + 0.01)
+        for k, o in enumerate(x_steps):
+            x_copy(ch, p, k, o).start()
+
     for ch in range(chunks):
-        own_copies[ch].wait()
-        for copy in z_copies[ch]:
+        front_own[ch].wait()
+        for copy in fronts[ch]:
             copy.wait_recv()
-
-        def features(i, carry, ch=ch):
-            rows = pl.ds(pl.multiple_of(i * tile, tile), tile)
-            delta = jnp.dot(sign[rows, :], recv[ch], preferred_element_type=jnp.float32)
-            square = delta * delta
-            total = square[:, :lanes] + square[:, lanes : 2 * lanes] + square[:, 2 * lanes :]
-            cols = pl.ds(pl.multiple_of((x * chunks + ch) * lanes, lanes), lanes)
-            out[rows, cols] = jnp.sqrt(total + 0.01)
-            for k, o in enumerate(x_steps):
-                x_copy(ch, i, k, o).start()
-            return carry
-
-        lax.fori_loop(0, tiles, features, 0)
+        delta = product(front_in[ch], sign[...], ((0,), (0,)))
+        square = delta * delta
+        third[...] = square[3 * part :]
+        keep(ch, 0, square[:part] + square[part : 2 * part] + square[2 * part : 3 * part])
         if ch == 0:
 
             @pl.when(x == 0)
             def _():
-                for i in range(tiles):
-                    first = out[i * tile : (i + 1) * tile, :lanes]
-                    edge[:, i * tile : (i + 1) * tile] = first.T[:HALO]
                 for k in range(feat_groups):
                     h_copy(k).start()
+
+        back_own[ch].wait()
+        for copy in backs[ch]:
+            copy.wait_recv()
+        delta = product(back_in[ch], sign[...], ((0,), (0,)))
+        square = delta * delta
+        keep(ch, 1, square[:part] + square[part:] + third[...])
 
     @pl.when(x == 0)
     def _():
@@ -174,52 +249,59 @@
 
     h_copy(0).wait_recv()
     for ch in range(chunks):
-        for copy in z_copies[ch]:
+        for copy in fronts[ch] + backs[ch]:
             copy.wait_send()
-
-        def finish(i, carry, ch=ch):
+        for p in range(2):
             for k, o in enumerate(x_steps):
-                x_copy(ch, i, k, o).wait()
-            return carry
-
-        lax.fori_loop(0, tiles, finish, 0)
-
-
-def exchange(coords, picked, slots, room, lanes, groups, feat_groups):
-    feats, width = slots.shape[0], picked.shape[1]
-    chunks = coords.shape[1] // (groups * feat_groups * lanes)
-    tile = min(256, feats)
+                x_copy(ch, p, k, o).wait()
+
+
+def exchange(coords, pairs, room, groups, feat_groups):
+    cols, width = pairs.shape[1], coords.shape[2]
+    feats = cols * feat_groups
+    chunks = coords.shape[1] // (groups * feat_groups * 128)
+    height = -(-groups * -(-width // 128) // 16) * 16
     vmem = pl.BlockSpec(memory_space=pltpu.VMEM)
     z_count, x_count = max(groups - 1, 1), max(feat_groups - 1, 1)
     dma = pltpu.SemaphoreType.DMA
     return pl.pallas_call(
-        functools.partial(exchange_kernel, groups, feat_groups, room, lanes, chunks, tile),
+        functools.partial(exchange_kernel, groups, feat_groups, room, chunks),
         out_shape=(
-            jax.ShapeDtypeStruct((feats, feat_groups * chunks * lanes), jnp.float32),
-            jax.ShapeDtypeStruct((HALO, feats // feat_groups), jnp.float32),
+            jax.ShapeDtypeStruct((feat_groups * chunks * 128, feats), jnp.float32),
+            jax.ShapeDtypeStruct((HALO, cols), jnp.float32),
+            jax.ShapeDtypeStruct((8, 128), jnp.float32),
         ),
-        in_specs=[pl.BlockSpec(memory_space=pl.ANY), vmem, vmem],
-        out_specs=(vmem, vmem),
+        in_specs=[pl.BlockSpec(memory_space=pl.ANY), vmem],
+        out_specs=(vmem, vmem, vmem),
         scratch_shapes=[
-            pltpu.VMEM((chunks, groups, 3, lanes, width), jnp.bfloat16),
+            pltpu.VMEM((chunks, groups, 3, 128, width), jnp.bfloat16),
+            pltpu.VMEM((feat_groups, 2, cols), jnp.int32),
+            pltpu.VMEM((height, 128), jnp.float32),
             pltpu.VMEM((room, width), jnp.bfloat16),
-            pltpu.VMEM((chunks, groups, room, 3 * lanes), jnp.bfloat16),
-            pltpu.VMEM((feats, groups * room), jnp.bfloat16),
-            pltpu.VMEM((chunks, groups * room, 3 * lanes), jnp.bfloat16),
-            pltpu.VMEM((HALO, feats), jnp.float32),
+            pltpu.VMEM((chunks, groups, room, 256), jnp.bfloat16),
+            pltpu.VMEM((chunks, groups, room, 128), jnp.bfloat16),
+            pltpu.VMEM((groups * room, feats), jnp.bfloat16),
+            pltpu.VMEM((chunks, groups * room, 256), jnp.bfloat16),
+            pltpu.VMEM((chunks, groups * room, 128), jnp.bfloat16),
+            pltpu.VMEM((64, feats), jnp.float32),
             dma((chunks, groups)),
+            dma((x_count,)),
+            dma((x_count,)),
+            dma((chunks, z_count)),
+            dma((chunks, z_count)),
             dma((chunks, z_count)),
             dma((chunks, z_count)),
             dma((chunks,)),
-            dma((chunks, feats // tile, x_count)),
-            dma((chunks, feats // tile, x_count)),
+            dma((chunks,)),
+            dma((chunks, 2, x_count)),
+            dma((chunks, 2, x_count)),
             dma((feat_groups,)),
             dma((1,)),
         ],
         compiler_params=pltpu.CompilerParams(
-            collective_id=0, has_side_effects=True, vmem_limit_bytes=48 * 1024 * 1024
+            collective_id=0, has_side_effects=True, vmem_limit_bytes=56 * 1024 * 1024
         ),
-    )(coords, picked, slots)
+    )(coords, pairs)
 
 
 def encode(inst, lag):
@@ -595,84 +677,96 @@
     )(every, halo, ids)
 
 
+def write_kernel(*refs):
+    count = len(refs) // 2
+    ins, outs, sem = refs[:count], refs[count:-1], refs[-1]
+    copies = [pltpu.make_async_copy(a, b, sem.at[i]) for i, (a, b) in enumerate(zip(ins, outs))]
+    for copy in copies:
+        copy.start()
+    for copy in copies:
+        copy.wait()
+
+
+def write_out(*arrays):
+    vmem, anywhere = pl.BlockSpec(memory_space=pltpu.VMEM), pl.BlockSpec(memory_space=pl.ANY)
+    return pl.pallas_call(
+        write_kernel,
+        out_shape=tuple(jax.ShapeDtypeStruct(a.shape, a.dtype) for a in arrays),
+        in_specs=[vmem] * len(arrays),
+        out_specs=(anywhere,) * len(arrays),
+        scratch_shapes=[pltpu.SemaphoreType.DMA((len(arrays),))],
+    )(*arrays)
+
+
 def slots_per_pass(width, refs, atoms):
     share = width * (1.0 - math.exp(-refs / atoms)) + 2.05 * math.sqrt(width)
     return min(-(-width // 16) * 16, -(-int(share) // 16) * 16)
 
 
+def collect(value, axis):
+    size = lax.axis_size(axis)
+    return lax.all_to_all(jnp.broadcast_to(value[None], (size,) + value.shape), axis, 0, 0, tiled=True)
+
+
+def plain(coords, atom_pairs, traj_ids):
+    groups, feat_groups, reps = lax.axis_size("atoms"), lax.axis_size("feat"), lax.axis_size("rep")
+    z, x = lax.axis_index("atoms"), lax.axis_index("feat")
+    width, cols = coords.shape[2], atom_pairs.shape[1]
+    frames = coords.shape[1] // groups
+    feats = cols * feat_groups
+    exact = lax.Precision.HIGHEST
+
+    split_up = jnp.transpose(coords.reshape(3, groups, frames, width), (1, 0, 2, 3))
+    got = lax.all_to_all(split_up, "atoms", 0, 0, tiled=True)
+    number = jnp.arange(groups * width, dtype=jnp.int32)[:, None]
+    sign = (number == atom_pairs[0]).astype(jnp.bfloat16) - (number == atom_pairs[1]).astype(jnp.bfloat16)
+    delta = matmul(got, sign.reshape(groups, width, cols), ((0, 3), (0, 1)))
+    own = jnp.sqrt(jnp.sum(delta * delta, 0) + 0.01)
+    every = jnp.transpose(collect(own, "feat"), (1, 0, 2)).reshape(frames, feats)
+    incoming = lax.ppermute(own[:LAG], "atoms", [(i, (i - 1) % groups) for i in range(groups)])
+    future = jnp.concatenate([own[LAG:], incoming], 0)
+    ids = jnp.concatenate([traj_ids[0], jnp.full((LAG,), -1, jnp.int32)])
+    now = lax.dynamic_slice_in_dim(ids, z * frames, frames)
+    later = lax.dynamic_slice_in_dim(ids, z * frames + LAG, frames)
+    valid = (now == later).astype(jnp.float32)[:, None]
+
+    def total(value):
+        return jnp.sum(collect(jnp.sum(collect(value, "rep"), 0), "atoms"), 0)
+
+    count = total(jnp.full((128,), jnp.sum(valid)))[0]
+    mean_now = total(jnp.sum(valid * every, 0)) / count
+    mean_next = total(jnp.sum(valid * future, 0)) / count
+    now_c, next_c = valid * (every - mean_now), valid * (future - mean_next)
+    scale_now = 1.0 / jnp.sqrt(total(jnp.sum(now_c * now_c, 0)) / count + 1e-05)
+    scale_next = 1.0 / jnp.sqrt(total(jnp.sum(next_c * next_c, 0)) / count + 1e-05)
+    own_c = lax.dynamic_slice_in_dim(now_c, x * cols, cols, 1)
+    own_scale = lax.dynamic_slice_in_dim(scale_now, x * cols, cols)
+    own_mean = lax.dynamic_slice_in_dim(mean_now, x * cols, cols)
+    local = matmul(now_c, jnp.concatenate([own_c, next_c], 1), ((0,), (0,)), exact)
+    rows = feats // (groups * reps)
+    local = local.reshape(groups, reps, rows, 2 * cols)
+    local = jnp.sum(lax.all_to_all(local, "atoms", 0, 0, tiled=True), 0)
+    mine = jnp.sum(lax.all_to_all(local, "rep", 0, 0, tiled=True), 0)
+    row = (z * reps + lax.axis_index("rep")) * rows
+    scale_rows = lax.dynamic_slice_in_dim(scale_now, row, rows)[:, None]
+    corr_inst = mine[:, :cols] / count * scale_rows * own_scale
+    corr_lag = mine[:, cols:] / count * scale_rows * scale_next
+    return corr_inst, corr_lag, (own - own_mean) * own_scale
+
+
 def shards(atom_coords, atom_pairs, traj_ids):
-    groups = lax.axis_size("atoms")
-    feat_groups = lax.axis_size("feat")
-    frames = atom_coords.shape[1]
-    frames_here = frames // groups
-    part = frames_here // feat_groups
+    groups, feat_groups, reps = lax.axis_size("atoms"), lax.axis_size("feat"), lax.axis_size("rep")
     width = atom_coords.shape[3]
-    cols = atom_pairs.shape[1]
-    z = lax.axis_index("atoms")
-    x = lax.axis_index("feat")
-
-    pairs = lax.all_gather(atom_pairs, "feat", axis=1, tiled=True)
-    feats = pairs.shape[1]
-    refs = pairs.reshape(-1)
-    room = slots_per_pass(width, 2 * feats, width * groups)
-
-    atom_no = jnp.arange(groups * width, dtype=jnp.int32).reshape(groups, width)
-    hit = atom_no[:, :, None] == refs[None, None, :]
-    used = jnp.any(hit, axis=2)
-    before = (jnp.arange(width)[:, None] < jnp.arange(width)[None, :]).astype(jnp.bfloat16)
-    rank = matmul(used.astype(jnp.bfloat16), before, ((1,), (0,)))
-    most = jnp.max(jnp.sum(used.astype(jnp.float32), 1))
-    ref_rank = jnp.sum(jnp.where(hit, rank[:, :, None], 0.0), axis=(0, 1)).reshape(2, feats)
-    ref_shard = pairs // width
-    used_own = lax.dynamic_index_in_dim(used, z, 0, False)
-    rank_own = lax.dynamic_index_in_dim(rank, z, 0, False)
-
+    room = slots_per_pass(width, 2 * atom_pairs.shape[1] * feat_groups, width * groups)
     coords = jnp.transpose(atom_coords[0], (1, 0, 2))
-    lanes = 128 if part % 128 == 0 else part
-    chunks = part // lanes
-
-    def spots(turn):
-        spot = ref_rank - turn * jnp.float32(room)
-        inside = (spot >= 0) & (spot < room)
-        return jnp.where(inside, ref_shard * room + spot.astype(jnp.int32), -1).T
-
-    def one_pass():
-        picked = jnp.where(used_own, rank_own.astype(jnp.int32), -1)[None]
-        return exchange(coords, picked, spots(jnp.float32(0.0)), room, lanes, groups, feat_groups)
-
-    def more_passes():
-        def step(carry):
-            turn, delta = carry
-            spot = spots(turn)
-            slot = jnp.arange(room, dtype=jnp.float32) + turn * jnp.float32(room)
-            pick = ((rank_own[None, :] == slot[:, None]) & used_own[None, :]).astype(jnp.bfloat16)
-            grouped = coords.reshape(3, groups, feat_groups, part, width)
-            blocks = lax.dynamic_index_in_dim(grouped, x, 2, False)
-            chosen = matmul(pick, blocks, ((1,), (3,))).astype(jnp.bfloat16)
-            chosen = jnp.transpose(chosen.reshape(room, 3, groups, chunks, lanes), (2, 3, 0, 1, 4))
-            chosen = chosen.reshape(groups, chunks, room, 3 * lanes)
-            got = lax.all_to_all(chosen, "atoms", split_axis=0, concat_axis=0, tiled=True)
-            got = jnp.transpose(got, (0, 2, 1, 3)).reshape(groups * room, chunks * 3 * lanes)
-            place = jnp.arange(groups * room, dtype=jnp.int32)
-            sign = (spot[:, :1] == place).astype(jnp.bfloat16) - (spot[:, 1:] == place).astype(jnp.bfloat16)
-            return turn + 1.0, delta + matmul(sign, got, ((1,), (0,)))
-
-        _, delta = lax.while_loop(
-            lambda c: c[0] * room < most,
-            step,
-            (jnp.float32(0.0), jnp.zeros((feats, chunks * 3 * lanes), jnp.float32)),
-        )
-        delta = delta.reshape(feats, chunks, 3, lanes)
-        computed = jnp.sqrt(jnp.sum(delta * delta, axis=2) + 0.01).reshape(feats, part)
-        both = jnp.zeros((feats, frames_here), jnp.float32)
-        for o in range(feat_groups):
-            turned = lax.ppermute(computed, "feat", [(i, (i + o) % feat_groups) for i in range(feat_groups)])
-            both = lax.dynamic_update_slice_in_dim(both, turned, ((x - o) % feat_groups) * part, 1)
-        first = lax.dynamic_slice_in_dim(both[:, :HALO], x * cols, cols, 0).T
-        return both, lax.ppermute(first, "atoms", [(i, (i - 1) % groups) for i in range(groups)])
-
-    every, incoming = lax.cond(most <= room, one_pass, more_passes)
-    corr_inst, corr_lag, projections = moments(every.T, incoming, traj_ids, groups, lax.axis_size("rep"))
+    every, halo, over = exchange(coords, atom_pairs, room, groups, feat_groups)
+    results = moments(every, halo, traj_ids, groups, reps)
+    corr_inst, corr_lag, projections = lax.cond(
+        over[0, 0] > 0.0,
+        lambda a: plain(coords, atom_pairs, traj_ids),
+        lambda a: write_out(*a),
+        results,
+    )
     return (corr_inst, corr_lag, projections[None])
 
 

time: 147 us -> 124 us (0.84)
  blocking collectives: 9.94 us -> 0 us
  other arithmetic: 7.88 us -> 0 us
  local copies, waits for them, and re-layouts: 8.79 us -> 1.21 us
  Pallas kernels: 118 us -> 121 us
    all_gather x1 -> x0, blocking collectives: 9.94 us -> none  [shards(): pairs = lax.all_gather(atom_pairs, 'feat', axis=1, tiled=True)]
    unnamed x5 -> x4, local copies, waits for them, and re-layouts: 6.43 us -> 0.01 us
    pallas_call x1, Pallas kernels: 68.6 us -> 74 us  [exchange(): pl.pallas_call(functools.partial(exchange_kernel, groups, feat_groups, ro...]
    pallas_call x1, Pallas kernels: 49.4 us -> 45.5 us  [moments(): pl.pallas_call(functools.partial(moments_kernel, groups, reps), out_shape...]
    reduce_or x1 -> x0, other arithmetic: 3.68 us -> none  [shards(): used = jnp.any(hit, axis=2)]
    reduce_sum x2 -> x0, other arithmetic: 3.1 us -> none  [the longest x1 2.98 us: shards(): jnp.sum(jnp.where(hit, rank[:, :, None], 0.0), axis=(0, 1))]
    pallas_call x1 -> x0, local copies, waits for them, and re-layouts: 1.88 us -> none  [exchange(): pl.pallas_call(functools.partial(exchange_kernel, groups, feat_groups, ro...]
where the time goes in v2:
time: 124 us
  Pallas kernels  121 us (98%)
  between operations  1.51 us (1%)
    pallas_call x1, Pallas kernels, exchange(): pl.pallas_call(functools.partial(exchange_kernel, groups, feat_groups, ro...  74 us
    pallas_call x1, Pallas kernels, moments(): pl.pallas_call(functools.partial(moments_kernel, groups, reps), out_shape...  45.5 us

profile of v2, /device:TPU:0, one launch (start us, length us, event | category | flops | bytes accessed | tf_op | source)
XLA Modules:
  0.0 123.7 jit_solution(7655574834433877311)
XLA Ops:
  0.6 0.0 copy-start.3
  0.6 74.0 %shard_map.60 = (f32[512,1024]{1,0:T(8,128)}, f32[16,512]{1,0:T(8,128)}, f32[8,128]{1,0:T(8,128)}) custom-call(bf16[3,2048,768]{2,1,0:T(8,128)(2,1)} %bitcast.63, s32[2,512]{1,0:T(2,128)} %pairs.1), custom_call_target="tpu_custom_call" | custom-call | tf_op jit(solution)/shard_map/pallas_call | solution.py:267
  74.6 0.0 copy-start.4
  74.6 1.2 slice.24
  76.5 0.0 copy-done.3
  76.5 45.5 %shard_map.61 = (f32[128,512]{1,0:T(8,128)S(1)}, f32[128,512]{1,0:T(8,128)S(1)}, f32[512,512]{1,0:T(8,128)S(1)}) custom-call(f32[512,1024]{1,0:T(8,128)} %get-tuple-element.32.every, f32[16,512]{1,0:T(8,128)} %get-tuple-element.33.halo, s32[1,2048]{1,0:T(1,128)S(1)} %copy-done.3), custom_call_target="tpu_custom_call" | custom-call | tf_op jit(solution)/shard_map/pallas_call | solution.py:640
  122.1 0.0 copy-done.4
  122.1 1.4 %conditional.1 = (f32[128,512]{1,0:T(8,128)}, f32[128,512]{1,0:T(8,128)}, f32[1,512,512]{2,1,0:T(8,128)}) conditional(s32[]{:T(128)} %bitcast.21, (f32[128,512]{1,0:T(8,128)S(1)}, f32[128,512]{1,0:T(8,128)S(1)}, f32[512,512]{1,0:T(8,128)S(1)}) %shard_map.61, (s32[1,2048]{1,0:T(1,128)S(1)}, s32[2,512]{1,0:T(2,128)S(1)}, ...), branch_computations={%region_0.0_spmd, %region_1.0_spmd} | conditional | flops 11298428928 | bytes 154175200 | solution.py:764
  122.1 1.2 branch_0_fun.1
Async XLA Ops:
  0.6 75.9 %copy-start.3 = (s32[1,2048]{1,0:T(1,128)S(1)}, s32[1,2048]{1,0:T(1,128)}, u32[]{:S(2)}) copy-start(s32[1,2048]{1,0:T(1,128)} %ids.1) | copy-start | bytes 24580
  74.6 47.4 %copy-start.4 = (s32[2,512]{1,0:T(2,128)S(1)}, s32[2,512]{1,0:T(2,128)}, u32[]{:S(2)}) copy-start(s32[2,512]{1,0:T(2,128)} %pairs.1) | copy-start | bytes 12292

commit v3 on v2

--- a/solution.py
+++ b/solution.py
@@ -11,6 +11,7 @@
 LAG = 10
 HALO = 16
 CODE = 32700.0
+PIECES = 2
 
 
 def matmul(left, right, dims, precision=None):
@@ -21,12 +22,16 @@
 MESH = pl.DeviceIdType.MESH
 
 
-def exchange_kernel(groups, feat_groups, room, chunks, coords, pairs, every, halo, over, *scratch):
+def program_kernel(groups, feat_groups, reps, room, chunks, coords, pairs, ids, inst, lag, proj, over, *scratch):
     (
-        blocks, everyone, ranks, pick, front, back, sign, front_in, back_in, third,
+        every, halo, blocks_in, everyone, ranks, pick, front, back, sign, front_in, back_in, third,
+        ext, vcol, left3, right3, local, core, stats, gathered, table, side, columns, scales,
+        sums, from_below, from_above,
         load, p_send, p_recv, f_send, f_recv, b_send, b_recv, f_own, b_own, x_send, x_recv, h_send, h_recv,
+        c_send, c_recv, s_own, s_send, s_recv, z_send, l_recv, r_recv,
     ) = scratch
-    z, x = lax.axis_index("atoms"), lax.axis_index("feat")
+    z, r, x = lax.axis_index("atoms"), lax.axis_index("rep"), lax.axis_index("feat")
+    peers = [(a, b) for a in range(groups) for b in range(reps) if (a, b) != (0, 0)]
     lanes, part = 128, 64
     width = coords.shape[2]
     feats, cols = every.shape[1], pairs.shape[1]
@@ -41,13 +46,17 @@
         for i, dest in enumerate(z_dests):
             start = pl.multiple_of(dest * frames_here + (x * chunks + ch) * lanes, 16)
             row.append(
-                pltpu.make_async_copy(coords.at[:, pl.ds(start, lanes), :], blocks.at[ch, i], load.at[ch, i])
+                pltpu.make_async_copy(coords.at[:, pl.ds(start, lanes), :], blocks_in.at[ch, i], load.at[ch, i])
             )
             row[-1].start()
         loads.append(row)
     barrier = pltpu.get_barrier_semaphore()
-    for o in z_steps:
-        pl.semaphore_signal(barrier, 1, device_id={"atoms": lax.rem(z + o, groups)}, device_id_type=MESH)
+
+    def peer(a, b):
+        return {"atoms": lax.rem(z + a, groups), "rep": lax.rem(r + b, reps)}
+
+    for a, b in peers:
+        pl.semaphore_signal(barrier, 1, device_id=peer(a, b), device_id_type=MESH)
     for o in x_steps:
         pl.semaphore_signal(barrier, 1, device_id={"feat": lax.rem(x + o, feat_groups)}, device_id_type=MESH)
     z_up, z_down = lax.rem(z + 1, groups), lax.rem(z + groups - 1, groups)
@@ -65,11 +74,11 @@
 
     @pl.when(x == 0)
     def _():
-        pl.semaphore_wait(barrier, len(z_steps) + 2 * len(x_steps))
+        pl.semaphore_wait(barrier, len(peers) + 2 * len(x_steps))
 
     @pl.when(x != 0)
     def _():
-        pl.semaphore_wait(barrier, len(z_steps) + len(x_steps) + 1)
+        pl.semaphore_wait(barrier, len(peers) + len(x_steps) + 1)
 
     pair_copies = []
     for k, o in enumerate(x_steps):
@@ -121,7 +130,7 @@
     )
     rank = product(used, earlier, ((1,), (0,))) + before
     most = jnp.max(product(ones(same), filled, ((1,), (0,))))
-    over[...] = jnp.where(jnp.broadcast_to(most, over.shape) > room, 1.0, 0.0)
+    over[0, 0] = most
     ranks[...] = jnp.where(counts > 0.5, rank, -1.0)
     whole = rank.astype(jnp.int32)
     parts = jnp.concatenate(
@@ -146,10 +155,10 @@
         def get(first):
             return product(pick[...], first, ((1,), (1,))).astype(jnp.bfloat16)
 
-        early = [blocks[ch, i, c, :part] for c in range(2)]
-        late = [blocks[ch, i, c, part:] for c in range(2)]
+        early = [blocks_in[ch, i, c, :part] for c in range(2)]
+        late = [blocks_in[ch, i, c, part:] for c in range(2)]
         front[ch, i, :, :lanes] = get(jnp.concatenate(early, 0))
-        front[ch, i, :, lanes:] = get(blocks[ch, i, 2])
+        front[ch, i, :, lanes:] = get(blocks_in[ch, i, 2])
         back[ch, i] = get(jnp.concatenate(late, 0))
 
     here = pl.ds(pl.multiple_of(z * room, 16), room)
@@ -242,113 +251,18 @@
         square = delta * delta
         keep(ch, 1, square[:part] + square[part:] + third[...])
 
-    @pl.when(x == 0)
-    def _():
-        for k in range(feat_groups):
-            h_copy(k).wait_send()
-
     h_copy(0).wait_recv()
     for ch in range(chunks):
-        for copy in fronts[ch] + backs[ch]:
-            copy.wait_send()
         for p in range(2):
             for k, o in enumerate(x_steps):
-                x_copy(ch, p, k, o).wait()
-
-
-def exchange(coords, pairs, room, groups, feat_groups):
-    cols, width = pairs.shape[1], coords.shape[2]
-    feats = cols * feat_groups
-    chunks = coords.shape[1] // (groups * feat_groups * 128)
-    height = -(-groups * -(-width // 128) // 16) * 16
-    vmem = pl.BlockSpec(memory_space=pltpu.VMEM)
-    z_count, x_count = max(groups - 1, 1), max(feat_groups - 1, 1)
-    dma = pltpu.SemaphoreType.DMA
-    return pl.pallas_call(
-        functools.partial(exchange_kernel, groups, feat_groups, room, chunks),
-        out_shape=(
-            jax.ShapeDtypeStruct((feat_groups * chunks * 128, feats), jnp.float32),
-            jax.ShapeDtypeStruct((HALO, cols), jnp.float32),
-            jax.ShapeDtypeStruct((8, 128), jnp.float32),
-        ),
-        in_specs=[pl.BlockSpec(memory_space=pl.ANY), vmem],
-        out_specs=(vmem, vmem, vmem),
-        scratch_shapes=[
-            pltpu.VMEM((chunks, groups, 3, 128, width), jnp.bfloat16),
-            pltpu.VMEM((feat_groups, 2, cols), jnp.int32),
-            pltpu.VMEM((height, 128), jnp.float32),
-            pltpu.VMEM((room, width), jnp.bfloat16),
-            pltpu.VMEM((chunks, groups, room, 256), jnp.bfloat16),
-            pltpu.VMEM((chunks, groups, room, 128), jnp.bfloat16),
-            pltpu.VMEM((groups * room, feats), jnp.bfloat16),
-            pltpu.VMEM((chunks, groups * room, 256), jnp.bfloat16),
-            pltpu.VMEM((chunks, groups * room, 128), jnp.bfloat16),
-            pltpu.VMEM((64, feats), jnp.float32),
-            dma((chunks, groups)),
-            dma((x_count,)),
-            dma((x_count,)),
-            dma((chunks, z_count)),
-            dma((chunks, z_count)),
-            dma((chunks, z_count)),
-            dma((chunks, z_count)),
-            dma((chunks,)),
-            dma((chunks,)),
-            dma((chunks, 2, x_count)),
-            dma((chunks, 2, x_count)),
-            dma((feat_groups,)),
-            dma((1,)),
-        ],
-        compiler_params=pltpu.CompilerParams(
-            collective_id=0, has_side_effects=True, vmem_limit_bytes=56 * 1024 * 1024
-        ),
-    )(coords, pairs)
-
-
-def encode(inst, lag):
-    def one(v):
-        root = v * lax.rsqrt(jnp.abs(v) + 1e-30)
-        return jnp.round(root * CODE).astype(jnp.int32)
-
-    return (one(inst) << 16) | (one(lag) & 0xFFFF)
-
-
-def decode(word):
-    def one(q):
-        root = q.astype(jnp.float32) * (1.0 / CODE)
-        return root * jnp.abs(root)
-
-    return one(word >> 16), one((word << 16) >> 16)
-
-
-def split(value):
-    high = value.astype(jnp.bfloat16)
-    return high, (value - high.astype(jnp.float32)).astype(jnp.bfloat16)
-
-
-def moments_kernel(
-    groups, reps, every, halo, ids, inst, lag, proj, ext, vcol, left3, right3, local, core, stats, gathered,
-    table, side, columns, scales, sums, from_below, from_above, *sems
-):
-    c_send, c_recv, s_own, s_send, s_recv, z_send, l_recv, r_recv = sems
-    z, r, x = lax.axis_index("atoms"), lax.axis_index("rep"), lax.axis_index("feat")
-    frames, feats = every.shape
-    cols = halo.shape[1]
-    rows = inst.shape[0]
-    blocks = groups * reps
+                x_copy(ch, p, k, o).wait_recv()
+
+    frames, rows, blocks = frames_here, inst.shape[0], groups * reps
     me = z * reps + r
-    peers = [(a, b) for a in range(groups) for b in range(reps) if (a, b) != (0, 0)]
-    barrier = pltpu.get_barrier_semaphore()
-
-    def peer(a, b):
-        return {"atoms": lax.rem(z + a, groups), "rep": lax.rem(r + b, reps)}
-
-    for a, b in peers:
-        pl.semaphore_signal(barrier, 1, device_id=peer(a, b), device_id_type=MESH)
-
-    here = ids[:, pl.ds(pl.multiple_of(z * frames, 128), frames)]
+    present = ids[:, pl.ds(pl.multiple_of(z * frames, 128), frames)]
     after = ids[:, pl.ds(pl.multiple_of(jnp.minimum(z + 1, groups - 1) * frames, 128), 128)]
     after = jnp.where(z == groups - 1, -1, after)
-    names = jnp.concatenate([here, after], 1).astype(jnp.float32)
+    names = jnp.concatenate([present, after], 1).astype(jnp.float32)
     names = jnp.broadcast_to(names, (8, frames + 128))
     later = pltpu.roll(names, frames + 128 - LAG, 1)
     valid = (names == later).astype(jnp.float32)[:, :frames]
@@ -398,13 +312,11 @@
         return carry[0] + fold(now * now), carry[1] + fold(later * later)
 
     now_sq, next_sq = lax.fori_loop(0, frames // step, second, zero)
-    stats[...] = jnp.zeros_like(stats)
     stats[0:1, :] = now_mean
     stats[1:2, :] = jnp.sum(now_sq, 0, keepdims=True)
     stats[2:3, :cols] = next_mean
-    stats[3:4, :cols] = jnp.sum(next_sq, 0, keepdims=True)
-    stats[4:5, :] = jnp.broadcast_to(count, (1, feats))
-    pl.semaphore_wait(barrier, len(peers))
+    stats[2:3, cols : 2 * cols] = jnp.sum(next_sq, 0, keepdims=True)
+    stats[3:4, :feats] = jnp.broadcast_to(count, (1, feats))
 
     own_stats = pltpu.make_async_copy(stats, gathered.at[me], s_own.at[0])
     own_stats.start()
@@ -435,7 +347,7 @@
     tile = max(128, reps * rows)
     tiles, inside = feats // tile, tile // (reps * rows)
 
-    def product(k, carry):
+    def multiply(k, carry):
         half = k // 2
         t = jnp.where(k % 2 == 0, tiles - 1 - half, half)
         at = pl.ds(pl.multiple_of(t * tile, tile), tile)
@@ -451,7 +363,7 @@
                 core_copy(d, b).start()
         return carry
 
-    lax.fori_loop(0, tiles, product, 0)
+    lax.fori_loop(0, tiles, multiply, 0)
 
     own_stats.wait()
     for copy in stat_copies:
@@ -461,20 +373,20 @@
     now_total = jnp.zeros((1, feats), jnp.float32)
     next_total = jnp.zeros((1, cols), jnp.float32)
     for b in range(blocks):
-        size = gathered[b, 4:5, :]
+        size = gathered[b, 3:4, :feats]
         total = total + size
-        now_total = now_total + size * gathered[b, 0:1, :]
+        now_total = now_total + size * gathered[b, 0:1, :feats]
         next_total = next_total + size[:, :cols] * gathered[b, 2:3, :cols]
     mean_now = now_total / total
     mean_next = next_total / total[:, :cols]
     now_spread = jnp.zeros((1, feats), jnp.float32)
     next_spread = jnp.zeros((1, cols), jnp.float32)
     for b in range(blocks):
-        size = gathered[b, 4:5, :]
-        off = gathered[b, 0:1, :] - mean_now
-        now_spread = now_spread + (gathered[b, 1:2, :] + size * off * off)
+        size = gathered[b, 3:4, :feats]
+        off = gathered[b, 0:1, :feats] - mean_now
+        now_spread = now_spread + (gathered[b, 1:2, :feats] + size * off * off)
         off = gathered[b, 2:3, :cols] - mean_next
-        next_spread = next_spread + (gathered[b, 3:4, :cols] + size[:, :cols] * off * off)
+        next_spread = next_spread + (gathered[b, 2:3, cols : 2 * cols] + size[:, :cols] * off * off)
     scale_now = 1.0 / jnp.sqrt(now_spread / total + 1e-05)
     scale_next = 1.0 / jnp.sqrt(next_spread / total[:, :cols] + 1e-05)
     root = 1.0 / jnp.sqrt(total)
@@ -483,25 +395,27 @@
     table[blocks + 2 : blocks + 3, :] = scale_now
     table[blocks + 3 :, :] = jnp.zeros((5, feats), jnp.float32)
     for b in range(blocks):
-        size = gathered[b, 4:5, :]
-        table[b : b + 1, :] = (gathered[b, 0:1, :] - mean_now) * (scale_now * root)
+        size = gathered[b, 3:4, :feats]
+        table[b : b + 1, :] = (gathered[b, 0:1, :feats] - mean_now) * (scale_now * root)
         side[b : b + 1, cols:] = (
             size[:, :cols] * (gathered[b, 2:3, :cols] - mean_next) * (scale_next * root[:, :cols])
         )
     for b in range(blocks):
-        side[b : b + 1, :cols] = gathered[b, 4:5, :cols] * table[b : b + 1, own]
+        side[b : b + 1, :cols] = gathered[b, 3:4, :cols] * table[b : b + 1, own]
     scales[0:1, :cols] = table[blocks : blocks + 1, own]
     scales[0:1, cols:] = scale_next * root[:, :cols]
     columns[...] = table[...].T
 
-    tall = min(rows, 32)
-
-    def hop(d, up):
+    tall = min(rows // PIECES, 32)
+    piece = rows // PIECES
+
+    def hop(d, s, up):
+        at = pl.ds(pl.multiple_of(s * piece, piece), piece)
         return pltpu.make_async_remote_copy(
-            src_ref=sums.at[d],
-            dst_ref=(from_below if up else from_above).at[d],
-            send_sem=z_send.at[d],
-            recv_sem=(l_recv if up else r_recv).at[d],
+            src_ref=sums.at[d, at],
+            dst_ref=(from_below if up else from_above).at[d, at],
+            send_sem=z_send.at[d, s],
+            recv_sem=(l_recv if up else r_recv).at[d, s],
             device_id={"atoms": lax.rem(z + (1 if up else groups - 1), groups)},
             device_id_type=MESH,
         )
@@ -518,11 +432,12 @@
         for b in range(1, reps):
             core_copy(d, b).wait_recv()
 
-    def send(d, up, relay):
+    def send(d, s, up, relay):
         if relay:
-            hop(d, up).wait_recv()
-
-        def body(i, carry):
+            hop(d, s, up).wait_recv()
+
+        def body(j, carry):
+            i = s * (piece // tall) + j
             at = pl.ds(pl.multiple_of(i * tall, tall), tall)
             value = mine(d, i)
             inst_part, lag_part = value[:, :cols], value[:, cols:]
@@ -532,39 +447,44 @@
             sums[d, at, :] = encode(inst_part, lag_part)
             return carry
 
-        lax.fori_loop(0, rows // tall, body, 0)
-        hop(d, up).start()
+        lax.fori_loop(0, piece // tall, body, 0)
+        hop(d, s, up).start()
 
     def chain(k, carry):
-        above, below = groups - 1 - k, k
+        below, s = k // PIECES, k % PIECES
+        above = groups - 1 - below
 
         @pl.when(z < above)
         def _():
-            wait_core(above)
+            @pl.when(s == 0)
+            def _():
+                wait_core(above)
 
             @pl.when(z == 0)
             def _():
-                send(above, True, False)
+                send(above, s, True, False)
 
             @pl.when(z > 0)
             def _():
-                send(above, True, True)
+                send(above, s, True, True)
 
         @pl.when(z > below)
         def _():
-            wait_core(below)
+            @pl.when(s == 0)
+            def _():
+                wait_core(below)
 
             @pl.when(z == groups - 1)
             def _():
-                send(below, False, False)
+                send(below, s, False, False)
 
             @pl.when(z < groups - 1)
             def _():
-                send(below, False, True)
+                send(below, s, False, True)
 
         return carry
 
-    lax.fori_loop(0, groups, chain, 0)
+    lax.fori_loop(0, groups * PIECES, chain, 0)
 
     wait_core(z)
 
@@ -592,16 +512,15 @@
     lax.fori_loop(0, frames // step, project, 0)
 
     def arrive(up):
-        hop(z, up).wait_recv()
-
-        def body(i, carry):
-            at = pl.ds(pl.multiple_of(i * tall, tall), tall)
+        def body(s, carry):
+            hop(z, s, up).wait_recv()
+            at = pl.ds(pl.multiple_of(s * piece, piece), piece)
             more = decode((from_below if up else from_above)[z, at, :])
             inst[at, :] = inst[at, :] + more[0]
             lag[at, :] = lag[at, :] + more[1]
             return carry
 
-        lax.fori_loop(0, rows // tall, body, 0)
+        lax.fori_loop(0, PIECES, body, 0)
 
     @pl.when(z > 0)
     def _():
@@ -617,64 +536,131 @@
 
         @pl.when(z < d)
         def _():
-            hop(d, True).wait_send()
+            for s in range(PIECES):
+                hop(d, s, True).wait_send()
 
         @pl.when(z > d)
         def _():
-            hop(d, False).wait_send()
+            for s in range(PIECES):
+                hop(d, s, False).wait_send()
 
         return carry
 
     lax.fori_loop(0, groups, finish, 0)
 
-
-def moments(every, halo, ids, groups, reps):
-    frames, feats = every.shape
-    cols = halo.shape[1]
+    @pl.when(x == 0)
+    def _():
+        for k in range(feat_groups):
+            h_copy(k).wait_send()
+
+    for ch in range(chunks):
+        for copy in fronts[ch] + backs[ch]:
+            copy.wait_send()
+        for p in range(2):
+            for k, o in enumerate(x_steps):
+                x_copy(ch, p, k, o).wait_send()
+
+
+def program(coords, pairs, ids, room, groups, feat_groups, reps):
+    cols, width = pairs.shape[1], coords.shape[2]
+    feats, frames = cols * feat_groups, coords.shape[1] // groups
+    chunks = frames // (feat_groups * 128)
+    height = -(-groups * -(-width // 128) // 16) * 16
     blocks = groups * reps
     rows = feats // blocks
     vmem = pl.BlockSpec(memory_space=pltpu.VMEM)
+    z_count, x_count, core_count = max(groups - 1, 1), max(feat_groups - 1, 1), max(reps - 1, 1)
+    others = max(blocks - 1, 1)
     dma = pltpu.SemaphoreType.DMA
-    others, others_core = max(blocks - 1, 1), max(reps - 1, 1)
-    word = pltpu.VMEM((groups, rows, cols), jnp.int32)
+    bf16, f32, i32 = jnp.bfloat16, jnp.float32, jnp.int32
+    memory = [
+        ((frames, feats), f32),
+        ((HALO, cols), f32),
+        ((chunks, groups, 3, 128, width), bf16),
+        ((feat_groups, 2, cols), i32),
+        ((height, 128), f32),
+        ((room, width), bf16),
+        ((chunks, groups, room, 256), bf16),
+        ((chunks, groups, room, 128), bf16),
+        ((groups * room, feats), bf16),
+        ((chunks, groups * room, 256), bf16),
+        ((chunks, groups * room, 128), bf16),
+        ((64, feats), f32),
+        ((frames + HALO, cols), f32),
+        ((frames, 8), f32),
+        ((3 * frames, feats), bf16),
+        ((3 * frames, 2 * cols), bf16),
+        ((groups, reps, rows, 2 * cols), f32),
+        ((core_count, groups, rows, 2 * cols), f32),
+        ((4, max(feats, 2 * cols)), f32),
+        ((blocks, 4, max(feats, 2 * cols)), f32),
+        ((blocks + 8, feats), f32),
+        ((blocks, 2 * cols), f32),
+        ((feats, blocks + 8), f32),
+        ((8, 2 * cols), f32),
+        ((groups, rows, cols), i32),
+        ((groups, rows, cols), i32),
+        ((groups, rows, cols), i32),
+    ]
+    signals = [
+        (chunks, groups),
+        (x_count,),
+        (x_count,),
+        (chunks, z_count),
+        (chunks, z_count),
+        (chunks, z_count),
+        (chunks, z_count),
+        (chunks,),
+        (chunks,),
+        (chunks, 2, x_count),
+        (chunks, 2, x_count),
+        (feat_groups,),
+        (1,),
+        (core_count, groups),
+        (core_count, groups),
+        (1,),
+        (others,),
+        (others,),
+        (groups, PIECES),
+        (groups, PIECES),
+        (groups, PIECES),
+    ]
     return pl.pallas_call(
-        functools.partial(moments_kernel, groups, reps),
+        functools.partial(program_kernel, groups, feat_groups, reps, room, chunks),
         out_shape=(
-            jax.ShapeDtypeStruct((rows, cols), jnp.float32),
-            jax.ShapeDtypeStruct((rows, cols), jnp.float32),
-            jax.ShapeDtypeStruct((frames, cols), jnp.float32),
+            jax.ShapeDtypeStruct((rows, cols), f32),
+            jax.ShapeDtypeStruct((rows, cols), f32),
+            jax.ShapeDtypeStruct((frames, cols), f32),
+            jax.ShapeDtypeStruct((1, 1), f32),
         ),
-        in_specs=[vmem, vmem, vmem],
-        out_specs=(vmem, vmem, vmem),
-        scratch_shapes=[
-            pltpu.VMEM((frames + HALO, cols), jnp.float32),
-            pltpu.VMEM((frames, 8), jnp.float32),
-            pltpu.VMEM((3 * frames, feats), jnp.bfloat16),
-            pltpu.VMEM((3 * frames, 2 * cols), jnp.bfloat16),
-            pltpu.VMEM((groups, reps, rows, 2 * cols), jnp.float32),
-            pltpu.VMEM((others_core, groups, rows, 2 * cols), jnp.float32),
-            pltpu.VMEM((8, feats), jnp.float32),
-            pltpu.VMEM((blocks, 8, feats), jnp.float32),
-            pltpu.VMEM((blocks + 8, feats), jnp.float32),
-            pltpu.VMEM((blocks, 2 * cols), jnp.float32),
-            pltpu.VMEM((feats, blocks + 8), jnp.float32),
-            pltpu.VMEM((8, 2 * cols), jnp.float32),
-            word,
-            word,
-            word,
-            dma((others_core, groups)),
-            dma((others_core, groups)),
-            dma((1,)),
-            dma((others,)),
-            dma((others,)),
-            dma((groups,)),
-            dma((groups,)),
-            dma((groups,)),
-        ],
+        in_specs=[pl.BlockSpec(memory_space=pl.ANY), vmem, vmem],
+        out_specs=(vmem, vmem, vmem, pl.BlockSpec(memory_space=pltpu.SMEM)),
+        scratch_shapes=[pltpu.VMEM(*m) for m in memory] + [dma(m) for m in signals],
         compiler_params=pltpu.CompilerParams(
-            collective_id=1, has_side_effects=True, vmem_limit_bytes=56 * 1024 * 1024
+            collective_id=0, has_side_effects=True, vmem_limit_bytes=60 * 1024 * 1024
         ),
-    )(every, halo, ids)
+    )(coords, pairs, ids)
+
+
+def encode(inst, lag):
+    def one(v):
+        root = v * lax.rsqrt(jnp.abs(v) + 1e-30)
+        return jnp.round(root * CODE).astype(jnp.int32)
+
+    return (one(inst) << 16) | (one(lag) & 0xFFFF)
+
+
+def decode(word):
+    def one(q):
+        root = q.astype(jnp.float32) * (1.0 / CODE)
+        return root * jnp.abs(root)
+
+    return one(word >> 16), one((word << 16) >> 16)
+
+
+def split(value):
+    high = value.astype(jnp.bfloat16)
+    return high, (value - high.astype(jnp.float32)).astype(jnp.bfloat16)
 
 
 def write_kernel(*refs):
@@ -699,7 +685,7 @@
 
 
 def slots_per_pass(width, refs, atoms):
-    share = width * (1.0 - math.exp(-refs / atoms)) + 2.05 * math.sqrt(width)
+    share = width * (1.0 - math.exp(-refs / atoms)) + 1.5 * math.sqrt(width)
     return min(-(-width // 16) * 16, -(-int(share) // 16) * 16)
 
 
@@ -759,10 +745,9 @@
     width = atom_coords.shape[3]
     room = slots_per_pass(width, 2 * atom_pairs.shape[1] * feat_groups, width * groups)
     coords = jnp.transpose(atom_coords[0], (1, 0, 2))
-    every, halo, over = exchange(coords, atom_pairs, room, groups, feat_groups)
-    results = moments(every, halo, traj_ids, groups, reps)
+    *results, over = program(coords, atom_pairs, traj_ids, room, groups, feat_groups, reps)
     corr_inst, corr_lag, projections = lax.cond(
-        over[0, 0] > 0.0,
+        over[0, 0] > room,
         lambda a: plain(coords, atom_pairs, traj_ids),
         lambda a: write_out(*a),
         results,

time: 124 us -> 115 us (0.927)
  Pallas kernels: 121 us -> 113 us
    pallas_call x2 -> x1, Pallas kernels: 120 us -> 112 us  [program(): pl.pallas_call(functools.partial(program_kernel, groups, feat_groups, rep...]
where the time goes in v3:
time: 115 us
  Pallas kernels  113 us (98%)
  between operations  1.54 us (1%)
    pallas_call x1, Pallas kernels, program(): pl.pallas_call(functools.partial(program_kernel, groups, feat_groups, rep...  112 us

profile of v3, /device:TPU:0, one launch (start us, length us, event | category | flops | bytes accessed | tf_op | source)
XLA Modules:
  0.0 114.5 jit_solution(256712185812655162)
XLA Ops:
  0.6 0.0 copy-start.3
  0.6 0.0 copy-start.4
  0.7 111.5 %shard_map.60 = (f32[128,512]{1,0:T(8,128)S(1)}, f32[128,512]{1,0:T(8,128)S(1)}, f32[512,512]{1,0:T(8,128)S(1)}, f32[1,1]{1,0:T(1,128)}) custom-call(bf16[3,2048,768]{2,1,0:T(8,128)(2,1)} %bitcast.63, s32[2,512]{1,0:T(2,128)} %pairs.1, s32[1,2048]{1,0:T(1,128)} %ids.1), custom_call_target="tpu_custom_call" | custom-call | tf_op jit(solution)/shard_map/pallas_call | solution.py:628
  112.9 0.0 copy-done.3
  112.9 0.0 copy-done.4
  112.9 1.4 %conditional.1 = (f32[128,512]{1,0:T(8,128)}, f32[128,512]{1,0:T(8,128)}, f32[1,512,512]{2,1,0:T(8,128)}) conditional(s32[]{:T(128)} %bitcast.21, (f32[128,512]{1,0:T(8,128)S(1)}, f32[128,512]{1,0:T(8,128)S(1)}, f32[512,512]{1,0:T(8,128)S(1)}) %tuple.17, (s32[1,2048]{1,0:T(1,128)S(1)}, s32[2,512]{1,0:T(2,128)S(1)}, ...), branch_computations={%region_0.0_spmd, %region_1.0_spmd} | conditional | flops 11298428928 | bytes 154175200 | solution.py:749
  112.9 1.2 %branch_0_fun.1 = (f32[128,512]{1,0:T(8,128)}, f32[128,512]{1,0:T(8,128)}, f32[512,512]{1,0:T(8,128)}) custom-call(f32[128,512]{1,0:T(8,128)S(1)} %get-tuple-element.16.refs_0_, f32[128,512]{1,0:T(8,128)S(1)} %get-tuple-element.17.refs_1_, f32[512,512]{1,0:T(8,128)S(1)} %get-tuple-element.18.refs_2_), custom_call_target="tpu_custom_call" | custom-call | tf_op jit(solution)/shard_map/cond/branch_0_fun/pallas_call | solution.py:678
Async XLA Ops:
  0.6 112.3 %copy-start.3 = (s32[1,2048]{1,0:T(1,128)S(1)}, s32[1,2048]{1,0:T(1,128)}, u32[]{:S(2)}) copy-start(s32[1,2048]{1,0:T(1,128)} %ids.1) | copy-start | bytes 24580
  0.6 112.3 %copy-start.4 = (s32[2,512]{1,0:T(2,128)S(1)}, s32[2,512]{1,0:T(2,128)}, u32[]{:S(2)}) copy-start(s32[2,512]{1,0:T(2,128)} %pairs.1) | copy-start | bytes 12292

commit v4 on v3

--- a/solution.py
+++ b/solution.py
@@ -450,12 +450,32 @@
         lax.fori_loop(0, piece // tall, body, 0)
         hop(d, s, up).start()
 
-    def chain(k, carry):
-        below, s = k // PIECES, k % PIECES
-        above = groups - 1 - below
-
-        @pl.when(z < above)
+    turn_above = PIECES * z
+    turn_below = PIECES * (groups - 1 - z) + jnp.where(z >= groups // 2, 1, 0)
+
+    def chain(turn, carry):
+        down, up = turn - turn_below, turn - turn_above
+
+        @pl.when((down >= 0) & (down < PIECES * z))
         def _():
+            below, s = down // PIECES, down % PIECES
+
+            @pl.when(s == 0)
+            def _():
+                wait_core(below)
+
+            @pl.when(z == groups - 1)
+            def _():
+                send(below, s, False, False)
+
+            @pl.when(z < groups - 1)
+            def _():
+                send(below, s, False, True)
+
+        @pl.when((up >= 0) & (up < PIECES * (groups - 1 - z)))
+        def _():
+            above, s = groups - 1 - up // PIECES, up % PIECES
+
             @pl.when(s == 0)
             def _():
                 wait_core(above)
@@ -468,23 +488,9 @@
             def _():
                 send(above, s, True, True)
 
-        @pl.when(z > below)
-        def _():
-            @pl.when(s == 0)
-            def _():
-                wait_core(below)
-
-            @pl.when(z == groups - 1)
-            def _():
-                send(below, s, False, False)
-
-            @pl.when(z < groups - 1)
-            def _():
-                send(below, s, False, True)
-
         return carry
 
-    lax.fori_loop(0, groups * PIECES, chain, 0)
+    lax.fori_loop(0, PIECES * (groups - 1) + 1, chain, 0)
 
     wait_core(z)
 

time: 115 us -> 105 us (0.913)
  Pallas kernels: 113 us -> 102 us
    pallas_call x1, Pallas kernels: 112 us -> 101 us  [program(): pl.pallas_call(functools.partial(program_kernel, groups, feat_groups, rep...]
where the time goes in v4:
time: 105 us; the launch traced here: 104 us
  Pallas kernels  102 us (97%)
  between operations  1.54 us (1%)
    pallas_call x1, Pallas kernels, program(): pl.pallas_call(functools.partial(program_kernel, groups, feat_groups, rep...  101 us

profile of v4, /device:TPU:0, one launch (start us, length us, event | category | flops | bytes accessed | tf_op | source)
XLA Modules:
  0.0 104.0 jit_solution(1895638248568440057)
XLA Ops:
  0.6 0.0 copy-start.3
  0.6 0.0 copy-start.4
  0.7 101.0 %shard_map.60 = (f32[128,512]{1,0:T(8,128)S(1)}, f32[128,512]{1,0:T(8,128)S(1)}, f32[512,512]{1,0:T(8,128)S(1)}, f32[1,1]{1,0:T(1,128)}) custom-call(bf16[3,2048,768]{2,1,0:T(8,128)(2,1)} %bitcast.63, s32[2,512]{1,0:T(2,128)} %pairs.1, s32[1,2048]{1,0:T(1,128)} %ids.1), custom_call_target="tpu_custom_call" | custom-call | tf_op jit(solution)/shard_map/pallas_call | solution.py:634
  102.4 0.0 copy-done.3
  102.4 0.0 copy-done.4
  102.4 1.4 %conditional.1 = (f32[128,512]{1,0:T(8,128)}, f32[128,512]{1,0:T(8,128)}, f32[1,512,512]{2,1,0:T(8,128)}) conditional(s32[]{:T(128)} %bitcast.21, (f32[128,512]{1,0:T(8,128)S(1)}, f32[128,512]{1,0:T(8,128)S(1)}, f32[512,512]{1,0:T(8,128)S(1)}) %tuple.17, (s32[1,2048]{1,0:T(1,128)S(1)}, s32[2,512]{1,0:T(2,128)S(1)}, ...), branch_computations={%region_0.0_spmd, %region_1.0_spmd} | conditional | flops 11298428928 | bytes 154175200 | solution.py:755
  102.4 1.2 %branch_0_fun.1 = (f32[128,512]{1,0:T(8,128)}, f32[128,512]{1,0:T(8,128)}, f32[512,512]{1,0:T(8,128)}) custom-call(f32[128,512]{1,0:T(8,128)S(1)} %get-tuple-element.16.refs_0_, f32[128,512]{1,0:T(8,128)S(1)} %get-tuple-element.17.refs_1_, f32[512,512]{1,0:T(8,128)S(1)} %get-tuple-element.18.refs_2_), custom_call_target="tpu_custom_call" | custom-call | tf_op jit(solution)/shard_map/cond/branch_0_fun/pallas_call | solution.py:684
Async XLA Ops:
  0.6 101.7 %copy-start.3 = (s32[1,2048]{1,0:T(1,128)S(1)}, s32[1,2048]{1,0:T(1,128)}, u32[]{:S(2)}) copy-start(s32[1,2048]{1,0:T(1,128)} %ids.1) | copy-start | bytes 24580
  0.6 101.7 %copy-start.4 = (s32[2,512]{1,0:T(2,128)S(1)}, s32[2,512]{1,0:T(2,128)}, u32[]{:S(2)}) copy-start(s32[2,512]{1,0:T(2,128)} %pairs.1) | copy-start | bytes 12292

commit v5 on v4

--- a/solution.py
+++ b/solution.py
@@ -25,7 +25,7 @@
 def program_kernel(groups, feat_groups, reps, room, chunks, coords, pairs, ids, inst, lag, proj, over, *scratch):
     (
         every, halo, blocks_in, everyone, ranks, pick, front, back, sign, front_in, back_in, third,
-        ext, vcol, left3, right3, local, core, stats, gathered, table, side, columns, scales,
+        shift, sums_now, sums_next, vcol, left3, right3, local, core, stats, gathered, table, side, columns, scales,
         sums, from_below, from_above,
         load, p_send, p_recv, f_send, f_recv, b_send, b_recv, f_own, b_own, x_send, x_recv, h_send, h_recv,
         c_send, c_recv, s_own, s_send, s_recv, z_send, l_recv, r_recv,
@@ -229,34 +229,6 @@
         for k, o in enumerate(x_steps):
             x_copy(ch, p, k, o).start()
 
-    for ch in range(chunks):
-        front_own[ch].wait()
-        for copy in fronts[ch]:
-            copy.wait_recv()
-        delta = product(front_in[ch], sign[...], ((0,), (0,)))
-        square = delta * delta
-        third[...] = square[3 * part :]
-        keep(ch, 0, square[:part] + square[part : 2 * part] + square[2 * part : 3 * part])
-        if ch == 0:
-
-            @pl.when(x == 0)
-            def _():
-                for k in range(feat_groups):
-                    h_copy(k).start()
-
-        back_own[ch].wait()
-        for copy in backs[ch]:
-            copy.wait_recv()
-        delta = product(back_in[ch], sign[...], ((0,), (0,)))
-        square = delta * delta
-        keep(ch, 1, square[:part] + square[part:] + third[...])
-
-    h_copy(0).wait_recv()
-    for ch in range(chunks):
-        for p in range(2):
-            for k, o in enumerate(x_steps):
-                x_copy(ch, p, k, o).wait_recv()
-
     frames, rows, blocks = frames_here, inst.shape[0], groups * reps
     me = z * reps + r
     present = ids[:, pl.ds(pl.multiple_of(z * frames, 128), frames)]
@@ -271,53 +243,181 @@
     vcol[...] = valid.T
 
     own = pl.ds(pl.multiple_of(x * cols, 128), cols)
-    ext[:frames, :] = every[:, own]
-    ext[frames:, :] = halo[...]
     step = 32
-
-    def moved(i):
-        wide = ext[pl.ds(pl.multiple_of(i * step, step), step + 16), :]
-        return pltpu.roll(wide, step + 16 - LAG, 0)[:step]
+    span = frames // (feat_groups * step)
+    early = max(4 * (chunks - 1) - 1, 0)
+    others_x = feat_groups - 1
+    sizes = [
+        feat_groups * early * step,
+        (span - early + others_x * (span - 3 - early)) * step,
+        others_x * 3 * step + 16,
+    ]
+    starts = [0, 3 * sizes[0], 3 * (sizes[0] + sizes[1])]
+    sums_now[...] = jnp.zeros_like(sums_now)
+    sums_next[...] = jnp.zeros_like(sums_next)
 
     def fold(value):
         return jnp.sum(value.reshape(step // 8, 8, value.shape[1]), 0)
 
-    def first(i, carry):
-        at = pl.ds(pl.multiple_of(i * step, step), step)
-        weight = vcol[at, :1]
-        return carry[0] + fold(every[at, :] * weight), carry[1] + fold(moved(i) * weight)
-
-    zero = (jnp.zeros((8, feats), jnp.float32), jnp.zeros((8, cols), jnp.float32))
-    now_sum, next_sum = lax.fori_loop(0, frames // step, first, zero)
-    now_mean = jnp.sum(now_sum, 0, keepdims=True) * inverse
-    next_mean = jnp.sum(next_sum, 0, keepdims=True) * inverse
-
-    def second(i, carry):
-        base = pl.multiple_of(i * step, step)
-        at, at1, at2 = pl.ds(base, step), pl.ds(base + frames, step), pl.ds(base + 2 * frames, step)
-        weight = vcol[at, :1]
-        now = (every[at, :] - now_mean) * weight
-        later = (moved(i) - next_mean) * weight
+    def put(stage, at, count_rows, now, later):
+        size, start = sizes[stage], starts[stage]
+        spot = [pl.ds(pl.multiple_of(start + n * size + at, 16), count_rows) for n in range(3)]
         high, low = split(now)
-        left3[at, :] = high
-        left3[at1, :] = high
-        left3[at2, :] = low
-        right3[at, :cols] = left3[at, own]
-        right3[at1, :cols] = left3[at2, own]
-        right3[at2, :cols] = left3[at, own]
+        left3[spot[0], :] = high
+        left3[spot[1], :] = high
+        left3[spot[2], :] = low
+        right3[spot[0], :cols] = left3[spot[0], own]
+        right3[spot[1], :cols] = left3[spot[2], own]
+        right3[spot[2], :cols] = left3[spot[0], own]
         high, low = split(later)
-        right3[at, cols:] = high
-        right3[at1, cols:] = low
-        right3[at2, cols:] = high
-        return carry[0] + fold(now * now), carry[1] + fold(later * later)
-
-    now_sq, next_sq = lax.fori_loop(0, frames // step, second, zero)
-    stats[0:1, :] = now_mean
-    stats[1:2, :] = jnp.sum(now_sq, 0, keepdims=True)
-    stats[2:3, :cols] = next_mean
-    stats[2:3, cols : 2 * cols] = jnp.sum(next_sq, 0, keepdims=True)
+        right3[spot[0], cols:] = high
+        right3[spot[1], cols:] = low
+        right3[spot[2], cols:] = high
+
+    def center(ranges):
+        shift[...] = jnp.zeros_like(shift)
+        amount = 0
+        for which, low, high in ranges:
+
+            def add(n, carry, which=which, low=low):
+                at = pl.ds(pl.multiple_of((which * span + low + n) * step, step), step)
+                shift[...] = shift[...] + fold(every[at, :])
+                return carry
+
+            lax.fori_loop(0, high - low, add, 0)
+            amount += (high - low) * step
+        mean = jnp.sum(shift[...], 0, keepdims=True) * (1.0 / amount)
+        shift[...] = jnp.broadcast_to(mean, shift.shape)
+
+    def gather(stage, ranges):
+        place = 0
+        for which, low, high in ranges:
+
+            def body(n, carry, which=which, low=low, place=place):
+                base = pl.multiple_of((which * span + low + n) * step, step)
+                at = pl.ds(base, step)
+                weight = vcol[at, :1]
+                now = (every[at, :] - shift[:1, :]) * weight
+                wide = every[pl.ds(base, step + 16), own]
+                moved = pltpu.roll(wide, step + 16 - LAG, 0)[:step]
+                later = (moved - shift[:1, own]) * weight
+                put(stage, (place + n) * step, step, now, later)
+                sums_now[:8, :] = sums_now[:8, :] + fold(now)
+                sums_now[8:, :] = sums_now[8:, :] + fold(now * now)
+                sums_next[:8, :] = sums_next[:8, :] + fold(later)
+                sums_next[8:, :] = sums_next[8:, :] + fold(later * later)
+                return carry
+
+            lax.fori_loop(0, high - low, body, 0)
+            place += high - low
+
+    def core_copy(d, b):
+        return pltpu.make_async_remote_copy(
+            src_ref=local.at[d, lax.rem(r + b, reps)],
+            dst_ref=core.at[b - 1, d],
+            send_sem=c_send.at[b - 1, d],
+            recv_sem=c_recv.at[b - 1, d],
+            device_id={"rep": lax.rem(r + b, reps)},
+            device_id_type=MESH,
+        )
+
+    tile = max(128, reps * rows)
+    tiles, inside = feats // tile, tile // (reps * rows)
+
+    def multiply(stage, fresh, final):
+        rows3 = slice(starts[stage], starts[stage] + 3 * sizes[stage])
+
+        def body(k, carry):
+            half = k // 2
+            t = jnp.where(k % 2 == 0, tiles - 1 - half, half)
+            at = pl.ds(pl.multiple_of(t * tile, tile), tile)
+            got = lax.dot_general(
+                left3[rows3, at], right3[rows3, :], (((0,), (0,)), ((), ())), preferred_element_type=jnp.float32
+            )
+            for j in range(inside):
+                d = t * inside + j
+                for b in range(reps):
+                    low = (j * reps + b) * rows
+                    value = got[low : low + rows]
+                    local[d, b] = value if fresh else local[d, b] + value
+                if final:
+                    for b in range(1, reps):
+                        core_copy(d, b).start()
+            return carry
+
+        lax.fori_loop(0, tiles, body, 0)
+
+    rivals = [lax.rem(x + o, feat_groups) for o in x_steps]
+
+    def arrived(ch, p):
+        for k, o in enumerate(x_steps):
+            x_copy(ch, p, k, o).wait_recv()
+
+    def stage_early():
+        for ch in range(chunks - 1):
+            for p in range(2):
+                arrived(ch, p)
+        ranges = [(k, 0, early) for k in range(feat_groups)]
+        center(ranges)
+        gather(0, ranges)
+        multiply(0, True, False)
+
+    for ch in range(chunks):
+        if ch == chunks - 1 and early > 0:
+            stage_early()
+        front_own[ch].wait()
+        for copy in fronts[ch]:
+            copy.wait_recv()
+        delta = product(front_in[ch], sign[...], ((0,), (0,)))
+        square = delta * delta
+        third[...] = square[3 * part :]
+        keep(ch, 0, square[:part] + square[part : 2 * part] + square[2 * part : 3 * part])
+        if ch == 0:
+
+            @pl.when(x == 0)
+            def _():
+                for k in range(feat_groups):
+                    h_copy(k).start()
+
+        back_own[ch].wait()
+        for copy in backs[ch]:
+            copy.wait_recv()
+        delta = product(back_in[ch], sign[...], ((0,), (0,)))
+        square = delta * delta
+        keep(ch, 1, square[:part] + square[part:] + third[...])
+
+    h_copy(0).wait_recv()
+    every[frames:, own] = halo[...]
+    if early == 0:
+        for ch in range(chunks - 1):
+            for p in range(2):
+                arrived(ch, p)
+    arrived(chunks - 1, 0)
+    ranges = [(x, early, span)] + [(k, early, span - 3) for k in rivals]
+    if early == 0:
+        center(ranges)
+    gather(1, ranges)
+    multiply(1, early == 0, False)
+    arrived(chunks - 1, 1)
+    gather(2, [(k, span - 3, span) for k in rivals])
+    now_off = jnp.sum(sums_now[:8, :], 0, keepdims=True) * inverse
+    next_off = jnp.sum(sums_next[:8, :], 0, keepdims=True) * inverse
+    root_count = jnp.sqrt(count)
+    top = lax.broadcasted_iota(jnp.int32, (16, 1), 0) == 0
+    now_row, next_row = now_off * root_count, next_off * root_count
+    put(2, sizes[2] - 16, 16, jnp.where(top, now_row, 0.0), jnp.where(top, -next_row, 0.0))
+    for n in range(3):
+        spot = slice(starts[2] + (n + 1) * sizes[2] - 16, starts[2] + (n + 1) * sizes[2])
+        right3[spot, :cols] = -right3[spot, :cols]
+    stats[0:1, :feats] = shift[:1, :] + now_off
+    stats[1:2, :feats] = jnp.maximum(
+        jnp.sum(sums_now[8:, :], 0, keepdims=True) - count * now_off * now_off, 0.0
+    )
+    stats[2:3, :cols] = shift[:1, own] + next_off
+    stats[2:3, cols : 2 * cols] = jnp.maximum(
+        jnp.sum(sums_next[8:, :], 0, keepdims=True) - count * next_off * next_off, 0.0
+    )
     stats[3:4, :feats] = jnp.broadcast_to(count, (1, feats))
-
     own_stats = pltpu.make_async_copy(stats, gathered.at[me], s_own.at[0])
     own_stats.start()
     stat_copies = []
@@ -334,36 +434,7 @@
         )
         stat_copies[-1].start()
 
-    def core_copy(d, b):
-        return pltpu.make_async_remote_copy(
-            src_ref=local.at[d, lax.rem(r + b, reps)],
-            dst_ref=core.at[b - 1, d],
-            send_sem=c_send.at[b - 1, d],
-            recv_sem=c_recv.at[b - 1, d],
-            device_id={"rep": lax.rem(r + b, reps)},
-            device_id_type=MESH,
-        )
-
-    tile = max(128, reps * rows)
-    tiles, inside = feats // tile, tile // (reps * rows)
-
-    def multiply(k, carry):
-        half = k // 2
-        t = jnp.where(k % 2 == 0, tiles - 1 - half, half)
-        at = pl.ds(pl.multiple_of(t * tile, tile), tile)
-        got = lax.dot_general(
-            left3[:, at], right3[...], (((0,), (0,)), ((), ())), preferred_element_type=jnp.float32
-        )
-        for j in range(inside):
-            d = t * inside + j
-            for b in range(reps):
-                low = (j * reps + b) * rows
-                local[d, b] = got[low : low + rows]
-            for b in range(1, reps):
-                core_copy(d, b).start()
-        return carry
-
-    lax.fori_loop(0, tiles, multiply, 0)
+    multiply(2, False, True)
 
     own_stats.wait()
     for copy in stat_copies:
@@ -508,11 +579,11 @@
 
     lax.fori_loop(0, rows // tall, settle, 0)
 
-    center, stretch = table[blocks + 1 : blocks + 2, own], table[blocks + 2 : blocks + 3, own]
+    middle, stretch = table[blocks + 1 : blocks + 2, own], table[blocks + 2 : blocks + 3, own]
 
     def project(i, carry):
         at = pl.ds(pl.multiple_of(i * step, step), step)
-        proj[at, :] = (ext[at, :] - center) * stretch
+        proj[at, :] = (every[at, own] - middle) * stretch
         return carry
 
     lax.fori_loop(0, frames // step, project, 0)
@@ -580,7 +651,7 @@
     dma = pltpu.SemaphoreType.DMA
     bf16, f32, i32 = jnp.bfloat16, jnp.float32, jnp.int32
     memory = [
-        ((frames, feats), f32),
+        ((frames + HALO, feats), f32),
         ((HALO, cols), f32),
         ((chunks, groups, 3, 128, width), bf16),
         ((feat_groups, 2, cols), i32),
@@ -592,10 +663,12 @@
         ((chunks, groups * room, 256), bf16),
         ((chunks, groups * room, 128), bf16),
         ((64, feats), f32),
-        ((frames + HALO, cols), f32),
+        ((8, feats), f32),
+        ((16, feats), f32),
+        ((16, cols), f32),
         ((frames, 8), f32),
-        ((3 * frames, feats), bf16),
-        ((3 * frames, 2 * cols), bf16),
+        ((3 * frames + 48, feats), bf16),
+        ((3 * frames + 48, 2 * cols), bf16),
         ((groups, reps, rows, 2 * cols), f32),
         ((core_count, groups, rows, 2 * cols), f32),
         ((4, max(feats, 2 * cols)), f32),

time: 105 us -> 102 us (0.971)
  Pallas kernels: 102 us -> 100 us
    pallas_call x1, Pallas kernels: 101 us -> 99 us  [program(): pl.pallas_call(functools.partial(program_kernel, groups, feat_groups, rep...]
where the time goes in v5:
time: 102 us
  Pallas kernels  100 us (98%)
  between operations  1.54 us (2%)
    pallas_call x1, Pallas kernels, program(): pl.pallas_call(functools.partial(program_kernel, groups, feat_groups, rep...  99 us

profile of v5, /device:TPU:0, one launch (start us, length us, event | category | flops | bytes accessed | tf_op | source)
XLA Modules:
  0.0 102.0 jit_solution(7082018074171964312)
XLA Ops:
  0.6 0.0 copy-start.3
  0.6 0.0 copy-start.4
  0.7 99.0 %shard_map.60 = (f32[128,512]{1,0:T(8,128)S(1)}, f32[128,512]{1,0:T(8,128)S(1)}, f32[512,512]{1,0:T(8,128)S(1)}, f32[1,1]{1,0:T(1,128)}) custom-call(bf16[3,2048,768]{2,1,0:T(8,128)(2,1)} %bitcast.63, s32[2,512]{1,0:T(2,128)} %pairs.1, s32[1,2048]{1,0:T(1,128)} %ids.1), custom_call_target="tpu_custom_call" | custom-call | tf_op jit(solution)/shard_map/pallas_call | solution.py:707
  100.4 0.0 copy-done.3
  100.4 0.0 copy-done.4
  100.4 1.4 %conditional.1 = (f32[128,512]{1,0:T(8,128)}, f32[128,512]{1,0:T(8,128)}, f32[1,512,512]{2,1,0:T(8,128)}) conditional(s32[]{:T(128)} %bitcast.21, (f32[128,512]{1,0:T(8,128)S(1)}, f32[128,512]{1,0:T(8,128)S(1)}, f32[512,512]{1,0:T(8,128)S(1)}) %tuple.17, (s32[1,2048]{1,0:T(1,128)S(1)}, s32[2,512]{1,0:T(2,128)S(1)}, ...), branch_computations={%region_0.0_spmd, %region_1.0_spmd} | conditional | flops 11298428928 | bytes 154175200 | solution.py:828
  100.4 1.2 %branch_0_fun.1 = (f32[128,512]{1,0:T(8,128)}, f32[128,512]{1,0:T(8,128)}, f32[512,512]{1,0:T(8,128)}) custom-call(f32[128,512]{1,0:T(8,128)S(1)} %get-tuple-element.16.refs_0_, f32[128,512]{1,0:T(8,128)S(1)} %get-tuple-element.17.refs_1_, f32[512,512]{1,0:T(8,128)S(1)} %get-tuple-element.18.refs_2_), custom_call_target="tpu_custom_call" | custom-call | tf_op jit(solution)/shard_map/cond/branch_0_fun/pallas_call | solution.py:757
Async XLA Ops:
  0.6 99.8 %copy-start.3 = (s32[1,2048]{1,0:T(1,128)S(1)}, s32[1,2048]{1,0:T(1,128)}, u32[]{:S(2)}) copy-start(s32[1,2048]{1,0:T(1,128)} %ids.1) | copy-start | bytes 24580
  0.6 99.8 %copy-start.4 = (s32[2,512]{1,0:T(2,128)S(1)}, s32[2,512]{1,0:T(2,128)}, u32[]{:S(2)}) copy-start(s32[2,512]{1,0:T(2,128)} %pairs.1) | copy-start | bytes 12292
